TPU v7x, 32 devices: a whole 2x2x4 slice. The times are simulated.
32 devices in a mesh: section: 2 (over x), tile: 8 (over z, core), slide: 2 (over y).
Axes of the slice: x: 2, y: 2, z: 4, core: 2. Of those that a mesh axis runs over, the one named last changes fastest.
Arguments:
- features: bfloat16 [2, 16384, 2048], P('slide', ('section', 'tile')), may hold values from -6 to 6
- w_proj: bfloat16 [2048, 1024], P(('section', 'tile', 'slide')), may hold values from -0.25 to 0.25
- w_fc: bfloat16 [1024, 128], replicated, may hold values from -0.1875 to 0.1875
- w_up: bfloat16 [3, 128, 256], replicated, may hold values from -0.5 to 0.5
- w_down: bfloat16 [3, 256, 128], replicated, may hold values from -0.375 to 0.375
- self_adj: bfloat16 [2, 128, 128, 128], P('slide', ('section', 'tile')), may hold values from -0.1875 to 0.1875
- adjacency: bfloat16 [2, 128, 8, 128, 128], P('slide', ('section', 'tile')), may hold values from -0.1875 to 0.1875
- nbr_block: int32 [2, 128, 8], P('slide'), may hold values from 0 to 127, as said below
- counts: int32 [2, 128], P('slide', ('section', 'tile')), may hold values from 6 to 8
Outputs:
- node_out: bfloat16 [2, 16384, 128], P('slide', ('section', 'tile'))
Inputs may be any that keep to these rules, and one draw needn't show every extreme that they name: `nbr_block`: block g of a slide is the (g % 8)-th block of the (g // 8)-th group of 8 blocks. Among the 64 entries of one such group, at most 4 name blocks of any one group, and some group is named exactly 4 times; slots beyond counts are named too.
All inputs are finite; a program needn't handle non-finite values.
Results may differ from a plain program's by a relative error of at most 0.015.
Values may be sent and summed in bfloat16 or wider, within the bound.
A program may use at most 64 MiB of HBM per device.

v0:
```python
import functools

import jax
import jax.numpy as jnp
from jax import lax
from jax.experimental import pallas as pl
from jax.experimental.pallas import tpu as pltpu
from jax.sharding import PartitionSpec as P

MESH = pl.DeviceIdType.MESH
CORES = 2
PARTS = 2
BF = jnp.bfloat16
F32 = jnp.float32


def remote(src, dst, send_sem, recv_sem, device):
    return pltpu.make_async_remote_copy(
        src_ref=src,
        dst_ref=dst,
        send_sem=send_sem,
        recv_sem=recv_sem,
        device_id=device,
        device_id_type=MESH,
    )


def greet(devices):
    barrier = pltpu.get_barrier_semaphore()
    for device in devices:
        pl.semaphore_signal(barrier, inc=1, device_id=device, device_id_type=MESH)
    return lambda: pl.semaphore_wait(barrier, len(devices))


def encode_kernel(tiles, x_hbm, w_ref, fc_hbm, out_ref, x_ref, fc_ref, w_all, acc, ld, z_s, z_r, xy_s, xy_r, dg_s, dg_r, pt_s, pt_r):
    zs = tiles // CORES
    far = zs // 2
    rows = w_ref.shape[0]
    half = rows // 2
    sx = lax.axis_index("section")
    sy = lax.axis_index("slide")
    t = lax.axis_index("tile")
    z, c = t // CORES, t % CORES
    ox, oy, oc = 1 - sx, 1 - sy, 1 - c
    oz = z + 1 - 2 * (z % 2)
    partner = {"tile": z * CORES + oc}
    xn, yn, zn = {"section": ox}, {"slide": oy}, {"tile": oz * CORES + c}
    places = [z] + [(z + 2 * j) % zs for j in range(1, far)] + [oz] + [(oz + 2 * j) % zs for j in range(1, far)]

    def zdev(j):
        return {"tile": ((z + 2 * j) % zs) * CORES + c}

    def at(x, m, core, y, k):
        start = ((x * tiles + places[m] * CORES + core) * 2 + y) * rows + k * half
        return w_all.at[pl.ds(pl.multiple_of(start, half), half)]

    started = []

    def go(src, dst, ss, rs, device):
        copy = remote(src, dst, ss, rs, device)
        copy.start()
        started.append(copy)

    def arrived(dst, ss, rs, device):
        remote(dst, dst, ss, rs, device).wait_recv()

    loads = [pltpu.make_async_copy(x_hbm, x_ref, ld.at[0]), pltpu.make_async_copy(fc_hbm, fc_ref, ld.at[1])]
    wait = greet([partner, xn, yn, zn] + [zdev(j) for j in range(1, far)])
    for load in loads:
        load.start()
    start = ((sx * tiles + t) * 2 + sy) * rows
    w_all[pl.ds(pl.multiple_of(start, rows), rows)] = w_ref[...]
    wait()

    def own(k):
        return w_ref.at[pl.ds(k * half, half)]

    for k in range(2):
        for j in range(1, far):
            go(own(k), at(sx, 0, c, sy, k), z_s.at[j, k], z_r.at[j, k], zdev(j))
    for k in range(2):
        go(own(k), at(sx, 0, c, sy, k), z_s.at[far, k], z_r.at[far, k], zn)

    def line(m, k):
        here = at(sx, m, c, sy, k)
        src = here if m else own(k)
        if 0 < m < far:
            arrived(here, z_s.at[0, k], z_r.at[far - m, k], zdev(m))
        elif m:
            arrived(here, z_s.at[0, k], z_r.at[m, k], zn)
        go(src, here, xy_s.at[0, m, k], xy_r.at[0, m, k], xn)
        go(src, here, xy_s.at[1, m, k], xy_r.at[1, m, k], yn)
        if 0 < m < far:
            go(src, here, z_s.at[far + m, k], z_r.at[far + m, k], zn)
        go(src, here, pt_s.at[0, m, k], pt_r.at[0, m, k], partner)

    def cross(m, k):
        for kind, device, other, ref in (
            (0, xn, yn, at(ox, m, c, sy, k)),
            (1, yn, xn, at(sx, m, c, oy, k)),
        ):
            arrived(ref, xy_s.at[kind, m, k], xy_r.at[kind, m, k], device)
            if k == kind:
                go(ref, ref, dg_s.at[m, k], dg_r.at[m, k], other)
            go(ref, ref, pt_s.at[1 + kind, m, k], pt_r.at[1 + kind, m, k], partner)

    def corner(m, k):
        ref = at(ox, m, c, oy, k)
        arrived(ref, dg_s.at[m, k], dg_r.at[m, k], (yn, xn)[k])
        go(ref, ref, pt_s.at[3, m, k], pt_r.at[3, m, k], partner)

    depth = CORES * 2 * rows
    tall = x_ref.shape[0] // 4

    def multiply(m):
        for k in range(2):
            for kind, (x, y) in enumerate(((sx, sy), (ox, sy), (sx, oy), (ox, oy))):
                arrived(at(x, m, oc, y, k), pt_s.at[kind, m, k], pt_r.at[kind, m, k], partner)
        slabs = [pl.ds(pl.multiple_of((x * zs + places[m]) * depth, depth), depth) for x in (sx, ox)]

        def body(i, carry):
            strip = pl.ds(pl.multiple_of(i * tall, tall), tall)
            total = jnp.dot(x_ref[strip, slabs[0]], w_all[slabs[0], :], preferred_element_type=F32)
            total += jnp.dot(x_ref[strip, slabs[1]], w_all[slabs[1], :], preferred_element_type=F32)
            if m:
                total += acc[strip, :]
            if m < zs - 1:
                acc[strip, :] = total
            else:
                enc = jnp.maximum(total, 0.0).astype(BF)
                out_ref[strip, :] = jnp.dot(enc, fc_ref[...], preferred_element_type=F32)
            return carry

        lax.fori_loop(0, 4, body, 0)

    steps = [(m, k) for m in range(zs) for k in range(2)]
    count = len(steps)
    for step in range(count + 5):
        if step < count:
            line(*steps[step])
        if 0 <= step - 2 < count:
            cross(*steps[step - 2])
        if 0 <= step - 4 < count:
            corner(*steps[step - 4])
        if step == 5:
            for load in loads:
                load.wait()
        if 0 <= step - 5 < count and steps[step - 5][1]:
            multiply(steps[step - 5][0])
    for copy in started:
        copy.wait_send()


def encode(rows, w_proj, w_fc):
    tiles = lax.axis_size("tile")
    zs = tiles // CORES
    vmem = pl.BlockSpec(memory_space=pltpu.VMEM)
    hbm = pl.BlockSpec(memory_space=pltpu.HBM)
    dma = pltpu.SemaphoreType.DMA
    return pl.pallas_call(
        functools.partial(encode_kernel, tiles),
        out_shape=jax.ShapeDtypeStruct((rows.shape[0], w_fc.shape[1]), F32),
        in_specs=[hbm, vmem, hbm],
        out_specs=vmem,
        scratch_shapes=[
            pltpu.VMEM(rows.shape, BF),
            pltpu.VMEM(w_fc.shape, BF),
            pltpu.VMEM((rows.shape[1], w_proj.shape[1]), BF),
            pltpu.VMEM((rows.shape[0], w_proj.shape[1]), F32),
            dma((2,)),
            dma((zs, 2)),
            dma((zs, 2)),
            dma((2, zs, 2)),
            dma((2, zs, 2)),
            dma((zs, 2)),
            dma((zs, 2)),
            dma((4, zs, 2)),
            dma((4, zs, 2)),
        ],
        compiler_params=pltpu.CompilerParams(
            collective_id=0, has_side_effects=True, vmem_limit_bytes=61 << 20
        ),
        name="encode",
    )(rows, w_proj, w_fc)


def hops_kernel(tiles, cap, parts, list_ref, state_ref, adj_ref, self_ref, up_ref, down_ref, out_ref,
                state, terms, send0, own0, recv0, send1, recv1, send2, recv2, send3, recv3, agg,
                s0, r0, s1, r1, s2, r2, s3, r3):
    hops = up_ref.shape[0]
    zs = tiles // CORES
    far = zs // 2
    blocks, slots, tb, _ = adj_ref.shape
    width = state_ref.shape[1]
    sends = blocks * slots
    per = blocks // parts
    chunks = zs * parts
    sx = lax.axis_index("section")
    t = lax.axis_index("tile")
    z, c = t // CORES, t % CORES
    ox, oc = 1 - sx, 1 - c
    oz = z + 1 - 2 * (z % 2)
    partner = {"tile": z * CORES + oc}
    xn = {"section": ox}
    zn = {"tile": oz * CORES + c}

    def zdev(j):
        return {"tile": ((z + 2 * j) % zs) * CORES + c}

    order = []
    for j in range(1, far):
        order += [(oz + 2 * j) % zs, (z + 2 * j) % zs]
    order += [oz, z]

    wait = greet([partner, xn, zn] + [zdev(j) for j in range(1, far)])
    terms[sends] = jnp.zeros((tb, width), BF)
    state[...] = state_ref[...]

    def term(b, carry):
        nodes = state[pl.ds(pl.multiple_of(b * tb, tb), tb), :].astype(BF)
        whole = jnp.dot(adj_ref[b].reshape(slots * tb, tb), nodes, preferred_element_type=F32)
        terms[pl.ds(b * slots, slots)] = whole.astype(BF).reshape(slots, tb, width)
        agg[pl.ds(pl.multiple_of(b * tb, tb), tb), :] = jnp.dot(self_ref[b], nodes, preferred_element_type=F32)
        return carry

    lax.fori_loop(0, blocks, term, 0)
    wait()

    for hop in range(hops):
        pending = []

        def go(src, dst, ss, rs, device):
            copy = remote(src, dst, ss, rs, device)
            copy.start()
            pending.append(copy)

        def arrived(dst, ss, rs, device):
            remote(dst, dst, ss, rs, device).wait_recv()

        def sums(dst, x, q, core):
            i, h = divmod(q, parts)
            first = ((x * zs + order[i]) * CORES + core) * blocks + h * per

            def body(r, carry):
                base = (first + r) * cap
                total = terms[list_ref[base]].astype(F32)
                for j in range(1, cap):
                    total += terms[list_ref[base + j]].astype(F32)
                dst[r] = total.astype(BF)
                return carry

            lax.fori_loop(0, per, body, 0)

        def chip(k, q):
            x = (ox, sx)[k]
            sums(send0.at[k, q], x, q, oc)
            go(send0.at[k, q], recv0.at[hop, k, q], s0.at[hop, k, q], r0.at[hop, k, q], partner)
            sums(own0.at[k, q], x, q, c)

        def pair(q):
            arrived(recv0.at[hop, 0, q], s0.at[hop, 0, q], r0.at[hop, 0, q], partner)

            def body(r, carry):
                send1[q, r] = (own0[0, q, r].astype(F32) + recv0[hop, 0, q, r].astype(F32)).astype(BF)
                return carry

            lax.fori_loop(0, per, body, 0)
            go(send1.at[q], recv1.at[hop, q], s1.at[hop, q], r1.at[hop, q], xn)

        chip(0, 0)
        for q in range(1, chunks):
            chip(0, q)
            pair(q - 1)
        chip(1, 0)
        pair(chunks - 1)
        for q in range(1, chunks):
            chip(1, q)

        for q in range(chunks):
            i, h = divmod(q, parts)
            arrived(recv0.at[hop, 1, q], s0.at[hop, 1, q], r0.at[hop, 1, q], partner)
            arrived(recv1.at[hop, q], s1.at[hop, q], r1.at[hop, q], xn)
            slot = (i // 2) * parts + h
            onward = i % 2 == 0
            if not onward:
                arrived(recv2.at[hop, slot], s2.at[hop, slot], r2.at[hop, slot], zn)
            home = i == zs - 1

            def gathered(r):
                total = own0[1, q, r].astype(F32) + recv0[hop, 1, q, r].astype(F32)
                total += recv1[hop, q, r].astype(F32)
                return total if onward else total + recv2[hop, slot, r].astype(F32)

            if not home:
                out = send2 if onward else send3

                def body(r, carry):
                    out[slot, r] = gathered(r).astype(BF)
                    return carry

                lax.fori_loop(0, per, body, 0)
                if onward:
                    go(send2.at[slot], recv2.at[hop, slot], s2.at[hop, slot], r2.at[hop, slot], zn)
                else:
                    go(send3.at[slot], recv3.at[hop, slot], s3.at[hop, slot], r3.at[hop, slot], zdev(i // 2 + 1))
                continue
            for j in range(1, far):
                there = (j - 1) * parts + h
                arrived(recv3.at[hop, there], s3.at[hop, there], r3.at[hop, there], zdev(j))

            def finish(r, carry):
                rows = pl.ds(pl.multiple_of((h * per + r) * tb, tb), tb)
                total = agg[rows, :] + gathered(r)
                for j in range(1, far):
                    total += recv3[hop, (j - 1) * parts + h, r].astype(F32)
                inner = jnp.dot(total.astype(BF), up_ref[hop], preferred_element_type=F32)
                inner = jnp.maximum(inner, 0.0).astype(BF)
                after = state[rows, :] + jnp.dot(inner, down_ref[hop], preferred_element_type=F32)
                if hop == hops - 1:
                    out_ref[rows, :] = after.astype(BF)
                else:
                    state[rows, :] = after
                return carry

            lax.fori_loop(0, per, finish, 0, unroll=True)
            if hop < hops - 1:
                lax.fori_loop(h * per, h * per + per, term, 0)
        for copy in pending:
            copy.wait_send()


def graph(state, adjacency, self_adj, w_up, w_down, lists, cap):
    tiles = lax.axis_size("tile")
    zs = tiles // CORES
    far = zs // 2
    blocks, slots, tb, _ = adjacency.shape
    width = state.shape[1]
    hops = w_up.shape[0]
    parts = PARTS if blocks % PARTS == 0 else 1
    piece = (blocks // parts, tb, width)
    chunks = zs * parts
    onward = far * parts
    distant = max(1, (far - 1) * parts)
    vmem = pl.BlockSpec(memory_space=pltpu.VMEM)
    dma = pltpu.SemaphoreType.DMA
    return pl.pallas_call(
        functools.partial(hops_kernel, tiles, cap, parts),
        out_shape=jax.ShapeDtypeStruct(state.shape, BF),
        in_specs=[pl.BlockSpec(memory_space=pltpu.SMEM)] + [vmem] * 5,
        out_specs=vmem,
        scratch_shapes=[
            pltpu.VMEM(state.shape, F32),
            pltpu.VMEM((blocks * slots + 1, tb, width), BF),
            pltpu.VMEM((2, chunks) + piece, BF),
            pltpu.VMEM((2, chunks) + piece, BF),
            pltpu.VMEM((hops, 2, chunks) + piece, BF),
            pltpu.VMEM((chunks,) + piece, BF),
            pltpu.VMEM((hops, chunks) + piece, BF),
            pltpu.VMEM((onward,) + piece, BF),
            pltpu.VMEM((hops, onward) + piece, BF),
            pltpu.VMEM((distant,) + piece, BF),
            pltpu.VMEM((hops, distant) + piece, BF),
            pltpu.VMEM(state.shape, F32),
        ]
        + [dma((hops, 2, chunks))] * 2
        + [dma((hops, chunks))] * 2
        + [dma((hops, onward))] * 2
        + [dma((hops, distant))] * 2,
        compiler_params=pltpu.CompilerParams(
            collective_id=1, has_side_effects=True, vmem_limit_bytes=50 << 20
        ),
        name="hops",
    )(lists, state, adjacency, self_adj, w_up, w_down)


def entry_lists(targets, live, total_blocks, cap):
    sends = targets.shape[0]
    positions = jnp.arange(sends, dtype=jnp.int32)
    same = (targets[:, None] == targets[None, :]) & live[None, :] & (positions[None, :] < positions[:, None])
    rank = jnp.sum(same.astype(jnp.int32), axis=1)
    hit = (jnp.arange(total_blocks, dtype=jnp.int32)[:, None, None] == targets[None, None, :]) & live[None, None, :]
    hit = hit & (jnp.arange(cap, dtype=jnp.int32)[None, :, None] == rank[None, None, :])
    found = jnp.sum(jnp.where(hit, positions[None, None, :] - sends, 0), axis=2) + sends
    return found.reshape(total_blocks * cap)


def local(features, w_proj, w_fc, w_up, w_down, self_adj, adjacency, nbr_block, counts):
    rows = features[0]
    blocks = self_adj.shape[1]
    tb = self_adj.shape[2]
    width = w_fc.shape[1]
    slots = adjacency.shape[2]
    hops = w_up.shape[0]
    pairs = lax.axis_size("section") == 2 and lax.axis_size("tile") % (2 * CORES) == 0
    peers = lax.axis_size("section") * lax.axis_size("tile")
    me_index = lax.axis_index("section") * lax.axis_size("tile") + lax.axis_index("tile")
    sends = blocks * slots
    cap = (sends + peers - 1) // peers
    if pairs and lax.axis_size("slide") == 2 and w_proj.shape[0] % 32 == 0:
        state = encode(rows, w_proj, w_fc)
    else:
        pre = jnp.dot(
            rows,
            lax.all_gather(w_proj, ("section", "tile", "slide"), axis=0, tiled=True),
            preferred_element_type=F32,
        )
        encoded = jax.nn.relu(pre).astype(BF)
        state = jnp.dot(encoded, w_fc, preferred_element_type=F32)
    live = jnp.arange(slots, dtype=jnp.int32)[None, :] < counts[0][:, None]
    if pairs and blocks <= CORES * cap:
        targets = lax.dynamic_slice_in_dim(nbr_block[0], me_index * blocks, blocks, 0).reshape(sends)
        lists = entry_lists(targets, live.reshape(sends), peers * blocks, cap)
        return graph(state, adjacency[0], self_adj[0], w_up, w_down, lists, cap)[None]
    table = nbr_block[0].reshape(peers, sends)
    target_dev = table // blocks
    target_local = table % blocks
    positions = jnp.arange(sends, dtype=jnp.int32)
    before = positions[None, :] < positions[:, None]
    same = target_dev[:, :, None] == target_dev[:, None, :]
    ranking = jnp.sum(jnp.logical_and(same, before[None]).astype(jnp.int32), axis=2)
    mine_dev = lax.dynamic_index_in_dim(target_dev, me_index, 0, keepdims=False)
    mine_rank = lax.dynamic_index_in_dim(ranking, me_index, 0, keepdims=False)
    slot_of = mine_dev * cap + mine_rank
    send_map = (jnp.arange(peers * cap, dtype=jnp.int32)[:, None] == slot_of[None, :]).astype(BF)
    arrive_hit = target_dev == me_index
    slot_flags = jnp.logical_and(
        arrive_hit[:, :, None],
        ranking[:, :, None] == jnp.arange(cap, dtype=jnp.int32)[None, None, :],
    ).astype(F32)
    local_flags = (
        target_local[:, :, None] == jnp.arange(blocks, dtype=jnp.int32)[None, None, :]
    ).astype(F32)
    recv_map = (
        jnp.einsum("pjc,pjr->rpc", slot_flags, local_flags).reshape(blocks, peers * cap).astype(BF)
    )
    for hop in range(hops):
        nodes = state.astype(BF).reshape(blocks, tb, width)
        own = jnp.einsum("bij,bjh->bih", self_adj[0], nodes, preferred_element_type=F32)
        terms = jnp.einsum("bkij,bjh->bkih", adjacency[0], nodes, preferred_element_type=F32)
        terms = (
            jnp.where(live[:, :, None, None], terms, 0.0).astype(BF).reshape(sends, tb * width)
        )
        outgoing = jnp.dot(send_map, terms, preferred_element_type=F32).astype(BF)
        outgoing = outgoing.reshape(peers, cap, tb, width)
        arrived = lax.all_to_all(
            outgoing, ("section", "tile"), split_axis=0, concat_axis=0, tiled=True
        )
        arrived = arrived.reshape(peers * cap, tb * width)
        incoming = jnp.dot(recv_map, arrived, preferred_element_type=F32).reshape(
            blocks, tb, width
        )
        gathered = (own + incoming).astype(BF).reshape(blocks * tb, width)
        inner = jax.nn.relu(jnp.dot(gathered, w_up[hop], preferred_element_type=F32)).astype(BF)
        state = state + jnp.dot(inner, w_down[hop], preferred_element_type=F32)
    return state.astype(BF)[None]


def solution(mesh):
    return jax.shard_map(
        local,
        mesh=mesh,
        in_specs=(
            P("slide", ("section", "tile"), None),
            P(("section", "tile", "slide"), None),
            P(),
            P(),
            P(),
            P("slide", ("section", "tile"), None, None),
            P("slide", ("section", "tile"), None, None, None),
            P("slide", None, None),
            P("slide", ("section", "tile")),
        ),
        out_specs=P("slide", ("section", "tile"), None),
        check_vma=False,
    )
```

profile of v0, /device:TPU:0, one launch (start us, length us, event | category | flops | bytes accessed | tf_op | source)
XLA Modules:
  0.0 130.5 jit_solution(14632057847235589961)
XLA Ops:
  0.0 0.0 copy-start
  0.0 0.0 copy-start.1
  0.0 0.0 copy-start.3
  0.0 0.0 copy-start.4
  0.0 0.9 iota_compare_fusion.2
  0.9 0.1 lt.47
  1.0 0.0 copy-done
  1.0 0.1 constant_dynamic-slice_fusion
  1.1 0.1 copy.12
  1.2 0.1 eq.52
  1.2 0.2 convert_reduce_fusion
  1.4 0.1 fusion
  1.5 0.1 select_reduce_fusion
  1.7 0.1 copy.13
  1.8 0.1 add.26.list_ref
  1.9 36.2 %encode.1.state_ref = f32[1024,128]{1,0:T(8,128)} custom-call(bf16[1024,2048]{1,0:T(8,128)(2,1)} %bitcast.8, bf16[64,1024]{1,0:T(8,128)(2,1)} %w_ref.1, bf16[1024,128]{1,0:T(8,128)(2,1)} %fc_hbm.1), custom_call_target="tpu_custom_call" | custom-call | tf_op jit(solution)/shard_map/encode/pallas_call | solution.py:160
  38.1 0.0 copy-done.1
  38.1 0.0 copy-done.3
  38.1 0.0 copy-done.5
  38.1 0.0 copy-done.4
  38.1 0.0 copy-start.2
  38.1 1.0 copy-done.2
  39.2 90.6 %hops.1 = bf16[1024,128]{1,0:T(8,128)(2,1)S(1)} custom-call(s32[512]{0:T(512)S(1)} %add.26.list_ref, f32[1024,128]{1,0:T(8,128)S(1)} %copy-done.2, bf16[8,8,128,128]{3,2,1,0:T(8,128)(2,1)S(1)} %bitcast.5, bf16[8,128,128]{2,1,0:T(8,128)(2,1)S(1)} %bitcast.7, bf16[3,128,256]{2,1,0:T(8,128)(2,1)S(1)} %copy-done.4, bf16[3,256,128]{2,1,0:T(8,128)(2,1)S(1)} %copy-done.5), custom_call_target="tpu_custom_call" | custom-call | tf_op jit(solution)/shard_map/hops/pallas_call | solution.py:346
  129.8 0.7 copy.15
  (4 shorter events, 0.0 us)
Async XLA Ops:
  0.0 1.0 copy-start
  0.0 38.1 %copy-start.1 = (bf16[1,8,8,128,128]{4,3,2,1,0:T(8,128)(2,1)S(1)}, bf16[1,8,8,128,128]{4,3,2,1,0:T(8,128)(2,1)}, u32[]{:S(2)}) copy-start(bf16[1,8,8,128,128]{4,3,2,1,0:T(8,128)(2,1)} %param.15) | copy-start | bytes 6291460
  0.0 38.1 %copy-start.3 = (bf16[1,8,128,128]{3,2,1,0:T(8,128)(2,1)S(1)}, bf16[1,8,128,128]{3,2,1,0:T(8,128)(2,1)}, u32[]{:S(2)}) copy-start(bf16[1,8,128,128]{3,2,1,0:T(8,128)(2,1)} %param.14) | copy-start | bytes 786436
  0.0 38.1 %copy-start.5 = (bf16[3,256,128]{2,1,0:T(8,128)(2,1)S(1)}, bf16[3,256,128]{2,1,0:T(8,128)(2,1)}, u32[]{:S(2)}) copy-start(bf16[3,256,128]{2,1,0:T(8,128)(2,1)} %down_ref.1) | copy-start | bytes 589828
  0.0 38.1 %copy-start.4 = (bf16[3,128,256]{2,1,0:T(8,128)(2,1)S(1)}, bf16[3,128,256]{2,1,0:T(8,128)(2,1)}, u32[]{:S(2)}) copy-start(bf16[3,128,256]{2,1,0:T(8,128)(2,1)} %up_ref.1) | copy-start | bytes 589828
  38.1 1.0 copy-start.2
where the time goes:
time: 131 us; the launch traced here: 130 us
  Pallas kernels  127 us (97%)
  local copies, waits for them, and re-layouts  2.3 us (2%)
    pallas_call x1, Pallas kernels, graph(): pl.pallas_call(functools.partial(hops_kernel, tiles, cap, parts), out_sha...  90.6 us
    pallas_call x1, Pallas kernels, encode(): pl.pallas_call(functools.partial(encode_kernel, tiles), out_shape=jax.Sha...  36.2 us

commit v1 on v0

v1 whole, which is shorter than its diff:
```python
import functools

import jax
import jax.numpy as jnp
from jax import lax
from jax.experimental import pallas as pl
from jax.experimental.pallas import tpu as pltpu
from jax.sharding import PartitionSpec as P

MESH = pl.DeviceIdType.MESH
CORES = 2
PARTS = 4
BF = jnp.bfloat16
F32 = jnp.float32


def remote(src, dst, send_sem, recv_sem, device):
    return pltpu.make_async_remote_copy(
        src_ref=src,
        dst_ref=dst,
        send_sem=send_sem,
        recv_sem=recv_sem,
        device_id=device,
        device_id_type=MESH,
    )


def greet(devices):
    barrier = pltpu.get_barrier_semaphore()
    for device in devices:
        pl.semaphore_signal(barrier, inc=1, device_id=device, device_id_type=MESH)
    return lambda: pl.semaphore_wait(barrier, len(devices))


def whole_kernel(tiles, cap, parts, hops, list_ref, x_hbm, w_ref, fc_hbm, adj_hbm, self_hbm, up_hbm, down_hbm, out_ref, *scratch):
    scratch = list(scratch)

    def take(count):
        taken = scratch[:count]
        del scratch[:count]
        return taken

    x_ref, fc_ref, w_all, acc, adj_ref, self_ref, up_ref, down_ref = take(8)
    pack, adj_e, adj_l, run_e, run_l, state, agg, mine, send1, send2 = take(10)
    nodes_e, nodes_l = take(hops), take(hops)
    recv1, recv2 = take(2)
    ld, z_s, z_r, xy_s, xy_r, dg_s, dg_r, pt_s, pt_r = take(9)
    aj_s, aj_r, nd_s, nd_r, s1, r1, s2, r2 = take(8)

    zs = tiles // CORES
    far = zs // 2
    rows = w_ref.shape[0]
    half = rows // 2
    blocks, tb, width = self_ref.shape[0], self_ref.shape[1], fc_ref.shape[1]
    sends = adj_ref.shape[0] - 1
    kinds = 2 * far
    batch = kinds * cap
    span = 2 * cap
    per = blocks // parts
    sx = lax.axis_index("section")
    sy = lax.axis_index("slide")
    t = lax.axis_index("tile")
    z, c = t // CORES, t % CORES
    ox, oy, oc = 1 - sx, 1 - sy, 1 - c
    oz = z + 1 - 2 * (z % 2)
    partner = {"tile": z * CORES + oc}
    xn, yn = {"section": ox}, {"slide": oy}
    zn, zp = {"tile": oz * CORES + c}, {"tile": oz * CORES + oc}
    places = [z] + [(z + 2 * j) % zs for j in range(1, far)] + [oz] + [(oz + 2 * j) % zs for j in range(1, far)]

    def zdev(j):
        return {"tile": ((z + 2 * j) % zs) * CORES + c}

    started = []

    def go(src, dst, ss, rs, device, log=started):
        copy = remote(src, dst, ss, rs, device)
        copy.start()
        log.append(copy)

    def arrived(dst, ss, rs, device):
        remote(dst, dst, ss, rs, device).wait_recv()

    loads = [
        pltpu.make_async_copy(src, dst, ld.at[i])
        for i, (src, dst) in enumerate(
            (
                (adj_hbm, adj_ref.at[pl.ds(0, sends)]),
                (x_hbm, x_ref),
                (fc_hbm, fc_ref),
                (self_hbm, self_ref),
                (up_hbm, up_ref),
                (down_hbm, down_ref),
            )
        )
    ]
    wait = greet([partner, xn, yn, zn, zp] + [zdev(j) for j in range(1, far)])
    for load in loads:
        load.start()
    start = ((sx * tiles + t) * 2 + sy) * rows
    w_all[pl.ds(pl.multiple_of(start, rows), rows)] = w_ref[...]
    adj_ref[sends] = jnp.zeros((tb, tb), BF)
    run_e[kinds * span] = jnp.zeros((tb, width), F32)
    run_l[kinds * span] = jnp.zeros((tb, width), F32)
    wait()

    def own(k):
        return w_ref.at[pl.ds(k * half, half)]

    def at(x, m, core, y, k):
        first = ((x * tiles + places[m] * CORES + core) * 2 + y) * rows + k * half
        return w_all.at[pl.ds(pl.multiple_of(first, half), half)]

    for k in range(2):
        for j in range(1, far):
            go(own(k), at(sx, 0, c, sy, k), z_s.at[j, k], z_r.at[j, k], zdev(j))
    for k in range(2):
        go(own(k), at(sx, 0, c, sy, k), z_s.at[far, k], z_r.at[far, k], zn)

    def line(m, k):
        here = at(sx, m, c, sy, k)
        src = here if m else own(k)
        if 0 < m < far:
            arrived(here, z_s.at[0, k], z_r.at[far - m, k], zdev(m))
        elif m:
            arrived(here, z_s.at[0, k], z_r.at[m, k], zn)
        go(src, here, xy_s.at[0, m, k], xy_r.at[0, m, k], xn)
        go(src, here, xy_s.at[1, m, k], xy_r.at[1, m, k], yn)
        if 0 < m < far:
            go(src, here, z_s.at[far + m, k], z_r.at[far + m, k], zn)
        go(src, here, pt_s.at[0, m, k], pt_r.at[0, m, k], partner)

    def cross(m, k):
        for kind, device, other, ref in (
            (0, xn, yn, at(ox, m, c, sy, k)),
            (1, yn, xn, at(sx, m, c, oy, k)),
        ):
            arrived(ref, xy_s.at[kind, m, k], xy_r.at[kind, m, k], device)
            if k == kind:
                go(ref, ref, dg_s.at[m, k], dg_r.at[m, k], other)
            go(ref, ref, pt_s.at[1 + kind, m, k], pt_r.at[1 + kind, m, k], partner)

    def corner(m, k):
        ref = at(ox, m, c, oy, k)
        arrived(ref, dg_s.at[m, k], dg_r.at[m, k], (yn, xn)[k])
        go(ref, ref, pt_s.at[3, m, k], pt_r.at[3, m, k], partner)

    def pack_tiles():
        def keep(i, carry):
            adj_e[i] = adj_ref[list_ref[i]]
            return carry

        def other(i, carry):
            pack[i] = adj_ref[list_ref[batch + i]]
            return carry

        lax.fori_loop(0, batch, keep, 0, unroll=4)
        lax.fori_loop(0, 3 * batch, other, 0, unroll=4)
        go(pack.at[pl.ds(0, batch)], adj_e.at[pl.ds(batch, batch)], aj_s.at[0, 0], aj_r.at[0, 0], partner)

    bit = batch // 2

    def send_tiles():
        for piece in range(2):
            for m, device in ((1, zn), (2, zp)):
                go(
                    pack.at[pl.ds(m * batch + piece * bit, bit)],
                    adj_l.at[pl.ds((m - 1) * batch + piece * bit, bit)],
                    aj_s.at[m, piece],
                    aj_r.at[m, piece],
                    device,
                )

    def nodes_out(hop, p):
        first = p * per
        here = nodes_e[hop].at[pl.ds(first, per)]
        go(here, nodes_e[hop].at[pl.ds(blocks + first, per)], nd_s.at[hop, 0, p], nd_r.at[hop, 0, p], partner)
        go(here, nodes_l[hop].at[pl.ds(first, per)], nd_s.at[hop, 1, p], nd_r.at[hop, 1, p], zn)

    depth = CORES * 2 * rows
    tall = per * tb

    def multiply(m):
        for k in range(2):
            for kind, (x, y) in enumerate(((sx, sy), (ox, sy), (sx, oy), (ox, oy))):
                arrived(at(x, m, oc, y, k), pt_s.at[kind, m, k], pt_r.at[kind, m, k], partner)
        slabs = [pl.ds(pl.multiple_of((x * zs + places[m]) * depth, depth), depth) for x in (sx, ox)]

        def product(strip):
            total = jnp.dot(x_ref[strip, slabs[0]], w_all[slabs[0], :], preferred_element_type=F32)
            return total + jnp.dot(x_ref[strip, slabs[1]], w_all[slabs[1], :], preferred_element_type=F32)

        if m < zs - 1:

            def body(i, carry):
                strip = pl.ds(pl.multiple_of(i * tall, tall), tall)
                total = product(strip)
                acc[strip, :] = total + acc[strip, :] if m else total
                return carry

            lax.fori_loop(0, parts, body, 0)
            return
        for p in range(parts):
            strip = pl.ds(p * tall, tall)
            enc = jnp.maximum(product(strip) + acc[strip, :], 0.0).astype(BF)
            first = jnp.dot(enc, fc_ref[...], preferred_element_type=F32)
            state[strip, :] = first
            nodes_e[0][pl.ds(p * per, per)] = first.astype(BF).reshape(per, tb, width)
            nodes_out(0, p)

    steps = [(m, k) for m in range(zs) for k in range(2)]
    count = len(steps)
    for step in range(count + 5):
        if step < count:
            line(*steps[step])
        if step == 1:
            loads[0].wait()
            pack_tiles()
        if step == 2 * far:
            send_tiles()
        if 0 <= step - 2 < count:
            cross(*steps[step - 2])
        if 0 <= step - 4 < count:
            corner(*steps[step - 4])
        if step == 5:
            for load in loads[1:]:
                load.wait()
        if 0 <= step - 5 < count and steps[step - 5][1]:
            multiply(steps[step - 5][0])

    at_a, at_n, at_k, at_l = (4 * batch + i * 2 * kinds * span for i in range(4))

    def runs(phase, k, hop):
        tiles_ref, nodes_ref, run = ((adj_e, nodes_e[hop], run_e), (adj_l, nodes_l[hop], run_l))[phase]
        total = None
        for i in range(span):
            e = (phase * kinds + k) * span + i
            one = jnp.dot(tiles_ref[list_ref[at_a + e]], nodes_ref[list_ref[at_n + e]], preferred_element_type=F32)
            total = one if total is None else total * list_ref[at_k + e].astype(F32) + one
            run[k * span + i] = total

    def block_sum(k, r):
        return run_e[list_ref[at_l + k * blocks + r]] + run_l[list_ref[at_l + (kinds + k) * blocks + r]]

    waiting = []
    for hop in range(hops):
        def own_block(b, carry):
            agg[b] = jnp.dot(self_ref[b], nodes_e[hop][b], preferred_element_type=F32)
            return carry

        lax.fori_loop(0, blocks, own_block, 0, unroll=2)
        for p in range(parts):
            ref = nodes_e[hop].at[pl.ds(blocks + p * per, per)]
            arrived(ref, nd_s.at[hop, 0, p], nd_r.at[hop, 0, p], partner)
        if hop == 0:
            ref = adj_e.at[pl.ds(batch, batch)]
            arrived(ref, aj_s.at[0, 0], aj_r.at[0, 0], partner)

        def early(k, carry):
            runs(0, k, hop)
            return carry

        lax.fori_loop(0, kinds, early, 0)
        for p in range(parts):
            ref = nodes_l[hop].at[pl.ds(p * per, per)]
            arrived(ref, nd_s.at[hop, 1, p], nd_r.at[hop, 1, p], zn)
            go(ref, nodes_l[hop].at[pl.ds(blocks + p * per, per)], nd_s.at[hop, 2, p], nd_r.at[hop, 2, p], partner)
        if hop == 0:
            for piece in range(2):
                for m, device in ((1, zn), (2, zp)):
                    ref = adj_l.at[pl.ds((m - 1) * batch + piece * bit, bit)]
                    arrived(ref, aj_s.at[m, piece], aj_r.at[m, piece], device)
        for p in range(parts):
            ref = nodes_l[hop].at[pl.ds(blocks + p * per, per)]
            arrived(ref, nd_s.at[hop, 2, p], nd_r.at[hop, 2, p], partner)

        for copy in waiting:
            copy.wait_send()
        waiting = []

        def across(j, k):
            runs(1, k, hop)
            for p in range(parts):
                for r in range(p * per, p * per + per):
                    send1[j, r] = block_sum(k, r).astype(BF)
                piece = pl.ds(p * per, per)
                go(send1.at[j, piece], recv1.at[hop, j, piece], s1.at[hop, j, p], r1.at[hop, j, p], xn, waiting)

        def crossed(j, p):
            ref = recv1.at[hop, j, pl.ds(p * per, per)]
            arrived(ref, s1.at[hop, j, p], r1.at[hop, j, p], xn)

        for j in range(1, far):
            across(j, 2 * j)
        for j in range(1, far):
            runs(1, 2 * j + 1, hop)
            for r in range(blocks):
                mine[j - 1, r] = block_sum(2 * j + 1, r)
        across(0, 0)
        runs(1, 1, hop)
        for r in range(blocks):
            agg[r] += block_sum(1, r)
        for p in range(parts):
            piece = pl.ds(p * per, per)
            for j in range(1, far):
                crossed(j, p)
                send2[j - 1, piece] = (mine[j - 1, piece] + recv1[hop, j, piece].astype(F32)).astype(BF)
                go(send2.at[j - 1, piece], recv2.at[hop, j - 1, piece], s2.at[hop, j - 1, p], r2.at[hop, j - 1, p], zdev(j), waiting)
        for p in range(parts):
            piece = pl.ds(p * per, per)
            strip = pl.ds(p * tall, tall)
            crossed(0, p)
            total = agg[piece] + recv1[hop, 0, piece].astype(F32)
            for j in range(1, far):
                arrived(recv2.at[hop, j - 1, piece], s2.at[hop, j - 1, p], r2.at[hop, j - 1, p], zdev(j))
                total += recv2[hop, j - 1, piece].astype(F32)
            gathered = total.astype(BF).reshape(tall, width)
            inner = jnp.dot(gathered, up_ref[hop], preferred_element_type=F32)
            inner = jnp.maximum(inner, 0.0).astype(BF)
            after = state[strip, :] + jnp.dot(inner, down_ref[hop], preferred_element_type=F32)
            if hop == hops - 1:
                out_ref[strip, :] = after.astype(BF)
            else:
                state[strip, :] = after
                nodes_e[hop + 1][piece] = after.astype(BF).reshape(per, tb, width)
                nodes_out(hop + 1, p)
    for copy in started + waiting:
        copy.wait_send()


def fused(rows, w_proj, w_fc, w_up, w_down, self_adj, adjacency, lists, cap):
    tiles = lax.axis_size("tile")
    zs = tiles // CORES
    far = zs // 2
    blocks, slots, tb, _ = adjacency.shape
    width = w_fc.shape[1]
    hops = w_up.shape[0]
    parts = PARTS if blocks % PARTS == 0 else 1
    kinds = 2 * far
    batch = kinds * cap
    span = 2 * cap
    distant = max(1, far - 1)
    vmem = pl.BlockSpec(memory_space=pltpu.VMEM)
    hbm = pl.BlockSpec(memory_space=pltpu.HBM)
    dma = pltpu.SemaphoreType.DMA
    tile = (tb, tb)
    piece = (blocks, tb, width)
    return pl.pallas_call(
        functools.partial(whole_kernel, tiles, cap, parts, hops),
        out_shape=jax.ShapeDtypeStruct((rows.shape[0], width), BF),
        in_specs=[pl.BlockSpec(memory_space=pltpu.SMEM), hbm, vmem] + [hbm] * 5,
        out_specs=vmem,
        scratch_shapes=[
            pltpu.VMEM(rows.shape, BF),
            pltpu.VMEM(w_fc.shape, BF),
            pltpu.VMEM((rows.shape[1], w_proj.shape[1]), BF),
            pltpu.VMEM((rows.shape[0], w_proj.shape[1]), F32),
            pltpu.VMEM((blocks * slots + 1,) + tile, BF),
            pltpu.VMEM(self_adj.shape, BF),
            pltpu.VMEM(w_up.shape, BF),
            pltpu.VMEM(w_down.shape, BF),
            pltpu.VMEM((3 * batch,) + tile, BF),
            pltpu.VMEM((2 * batch,) + tile, BF),
            pltpu.VMEM((2 * batch,) + tile, BF),
            pltpu.VMEM((kinds * span + 1, tb, width), F32),
            pltpu.VMEM((kinds * span + 1, tb, width), F32),
            pltpu.VMEM((rows.shape[0], width), F32),
            pltpu.VMEM(piece, F32),
            pltpu.VMEM((distant,) + piece, F32),
            pltpu.VMEM((far,) + piece, BF),
            pltpu.VMEM((distant,) + piece, BF),
        ]
        + [pltpu.VMEM((2 * blocks, tb, width), BF)] * (2 * hops)
        + [pltpu.VMEM((hops, far) + piece, BF), pltpu.VMEM((hops, distant) + piece, BF)]
        + [dma((6,))]
        + [dma((zs, 2))] * 2
        + [dma((2, zs, 2))] * 2
        + [dma((zs, 2))] * 2
        + [dma((4, zs, 2))] * 2
        + [dma((3, 2))] * 2
        + [dma((hops, 3, parts))] * 2
        + [dma((hops, far, parts))] * 2
        + [dma((hops, distant, parts))] * 2,
        compiler_params=pltpu.CompilerParams(
            collective_id=0, has_side_effects=True, vmem_limit_bytes=62 << 20
        ),
        name="whole",
    )(lists, rows, w_proj, w_fc, adjacency.reshape((blocks * slots,) + tile), self_adj, w_up, w_down)


def tile_lists(neighbours, counts, slots, cap):
    tiles = lax.axis_size("tile")
    zs = tiles // CORES
    far = zs // 2
    kinds = 2 * far
    span = 2 * cap
    blocks = counts.shape[0]
    sends = blocks * slots
    x = lax.axis_index("section")
    t = lax.axis_index("tile")
    z, c = t // CORES, t % CORES
    oz = z + 1 - 2 * (z % 2)
    seats = [(z, c), (z, 1 - c), (oz, c), (oz, 1 - c)]
    entries = neighbours.reshape(-1)

    def group(gx, gz, gc):
        return gx * tiles + gz * CORES + gc

    def receivers(seat):
        gz, gc = seat
        return [group(gx, (gz + 2 * j) % zs, gc) for j in range(far) for gx in (1 - x, x)]

    named = jnp.stack(
        [lax.dynamic_slice_in_dim(entries, group(x, gz, gc) * sends, sends) for gz, gc in seats]
    )
    place = jnp.arange(sends, dtype=jnp.int32)
    key = named * sends + place
    rank = jnp.sum((key[:, None, :] < key[:, :, None]).astype(jnp.int32), axis=2)
    live = (jnp.arange(slots, dtype=jnp.int32)[None, :] < counts[:, None]).reshape(sends)
    wanted = jnp.stack([g for seat in seats for g in receivers(seat)])
    wanted = (wanted[:, None] * cap + jnp.arange(cap, dtype=jnp.int32)[None, :]).reshape(-1)
    hit = (wanted[:, None] == rank[0][None, :]) & live[None, :]
    packed = sends + jnp.sum(jnp.where(hit, place[None, :] - sends, 0), axis=1)

    both = named.reshape(2, 2 * sends)
    seat_of = jnp.arange(2 * sends, dtype=jnp.int32) // sends
    key = both * (2 * sends) + jnp.arange(2 * sends, dtype=jnp.int32)
    order = jnp.sum((key[:, None, :] < key[:, :, None]).astype(jnp.int32), axis=2)
    tile_at = seat_of * (kinds * cap) + rank.reshape(2, 2 * sends) - (both // blocks) * cap
    node_at = jnp.arange(2 * sends, dtype=jnp.int32) // slots
    code = ((tile_at * (2 * blocks)) + node_at) * blocks + both % blocks
    mine = jnp.stack(receivers(seats[0]))
    ask = (mine[:, None] * span + jnp.arange(span, dtype=jnp.int32)[None, :]).reshape(-1)
    hit = ask[None, :, None] == order[:, None, :]
    code = jnp.sum(jnp.where(hit, code[:, None, :], 0), axis=2).reshape(2, kinds, span)
    block = code % blocks
    node = (code // blocks) % (2 * blocks)
    kind = jnp.arange(kinds, dtype=jnp.int32)[None, :, None]
    tile = code // (2 * blocks * blocks) + kind * cap
    first = jnp.arange(span, dtype=jnp.int32)[None, None, :] > 0
    same = first & (block == jnp.roll(block, 1, axis=2))
    want = jnp.arange(blocks, dtype=jnp.int32)[None, None, :, None]
    upto = jnp.sum((block[:, :, None, :] <= want).astype(jnp.int32), axis=3)
    there = jnp.any(block[:, :, None, :] == want, axis=3)
    last = jnp.where(there, kind * span + upto - 1, kinds * span)
    return jnp.concatenate(
        [packed, tile.reshape(-1), node.reshape(-1), same.astype(jnp.int32).reshape(-1), last.reshape(-1)]
    )


def local(features, w_proj, w_fc, w_up, w_down, self_adj, adjacency, nbr_block, counts):
    rows = features[0]
    blocks = self_adj.shape[1]
    tb = self_adj.shape[2]
    width = w_fc.shape[1]
    slots = adjacency.shape[2]
    hops = w_up.shape[0]
    peers = lax.axis_size("section") * lax.axis_size("tile")
    me_index = lax.axis_index("section") * lax.axis_size("tile") + lax.axis_index("tile")
    sends = blocks * slots
    cap = (sends + peers - 1) // peers
    live = jnp.arange(slots, dtype=jnp.int32)[None, :] < counts[0][:, None]
    square = lax.axis_size("section") == 2 and lax.axis_size("slide") == 2
    pairs = lax.axis_size("tile") % (2 * CORES) == 0
    if square and pairs and sends == peers * cap and w_proj.shape[0] % 32 == 0:
        lists = tile_lists(nbr_block[0], counts[0], slots, cap)
        return fused(rows, w_proj, w_fc, w_up, w_down, self_adj[0], adjacency[0], lists, cap)[None]
    pre = jnp.dot(
        rows,
        lax.all_gather(w_proj, ("section", "tile", "slide"), axis=0, tiled=True),
        preferred_element_type=F32,
    )
    encoded = jax.nn.relu(pre).astype(BF)
    state = jnp.dot(encoded, w_fc, preferred_element_type=F32)
    table = nbr_block[0].reshape(peers, sends)
    target_dev = table // blocks
    target_local = table % blocks
    positions = jnp.arange(sends, dtype=jnp.int32)
    before = positions[None, :] < positions[:, None]
    same = target_dev[:, :, None] == target_dev[:, None, :]
    ranking = jnp.sum(jnp.logical_and(same, before[None]).astype(jnp.int32), axis=2)
    mine_dev = lax.dynamic_index_in_dim(target_dev, me_index, 0, keepdims=False)
    mine_rank = lax.dynamic_index_in_dim(ranking, me_index, 0, keepdims=False)
    slot_of = mine_dev * cap + mine_rank
    send_map = (jnp.arange(peers * cap, dtype=jnp.int32)[:, None] == slot_of[None, :]).astype(BF)
    arrive_hit = target_dev == me_index
    slot_flags = jnp.logical_and(
        arrive_hit[:, :, None],
        ranking[:, :, None] == jnp.arange(cap, dtype=jnp.int32)[None, None, :],
    ).astype(F32)
    local_flags = (
        target_local[:, :, None] == jnp.arange(blocks, dtype=jnp.int32)[None, None, :]
    ).astype(F32)
    recv_map = (
        jnp.einsum("pjc,pjr->rpc", slot_flags, local_flags).reshape(blocks, peers * cap).astype(BF)
    )
    for hop in range(hops):
        nodes = state.astype(BF).reshape(blocks, tb, width)
        own = jnp.einsum("bij,bjh->bih", self_adj[0], nodes, preferred_element_type=F32)
        terms = jnp.einsum("bkij,bjh->bkih", adjacency[0], nodes, preferred_element_type=F32)
        terms = (
            jnp.where(live[:, :, None, None], terms, 0.0).astype(BF).reshape(sends, tb * width)
        )
        outgoing = jnp.dot(send_map, terms, preferred_element_type=F32).astype(BF)
        outgoing = outgoing.reshape(peers, cap, tb, width)
        arrived = lax.all_to_all(
            outgoing, ("section", "tile"), split_axis=0, concat_axis=0, tiled=True
        )
        arrived = arrived.reshape(peers * cap, tb * width)
        incoming = jnp.dot(recv_map, arrived, preferred_element_type=F32).reshape(
            blocks, tb, width
        )
        gathered = (own + incoming).astype(BF).reshape(blocks * tb, width)
        inner = jax.nn.relu(jnp.dot(gathered, w_up[hop], preferred_element_type=F32)).astype(BF)
        state = state + jnp.dot(inner, w_down[hop], preferred_element_type=F32)
    return state.astype(BF)[None]


def solution(mesh):
    return jax.shard_map(
        local,
        mesh=mesh,
        in_specs=(
            P("slide", ("section", "tile"), None),
            P(("section", "tile", "slide"), None),
            P(),
            P(),
            P(),
            P("slide", ("section", "tile"), None, None),
            P("slide", ("section", "tile"), None, None, None),
            P("slide", None, None),
            P("slide", ("section", "tile")),
        ),
        out_specs=P("slide", ("section", "tile"), None),
        check_vma=False,
    )
```

time: 131 us -> 118 us (0.901)
  Pallas kernels: 127 us -> 111 us
  local copies, waits for them, and re-layouts: 2.3 us -> 4.49 us
    pallas_call x2 -> x1, Pallas kernels: 127 us -> 111 us  [fused(): pl.pallas_call(functools.partial(whole_kernel, tiles, cap, parts, hops),...]
where the time goes in v1:
time: 118 us
  Pallas kernels  111 us (94%)
  local copies, waits for them, and re-layouts  4.49 us (4%)
  other arithmetic  2.43 us (2%)
    pallas_call x1, Pallas kernels, fused(): pl.pallas_call(functools.partial(whole_kernel, tiles, cap, parts, hops),...  111 us
    unnamed x2, local copies, waits for them, and re-layouts  2.46 us

profile of v1, /device:TPU:0, one launch (start us, length us, event | category | flops | bytes accessed | tf_op | source)
XLA Modules:
  0.0 118.0 jit_solution(295895067656408829)
XLA Ops:
  0.0 0.1 stack.89
  0.2 0.1 and.169
  0.3 0.7 iota_compare_fusion.2
  1.0 0.1 lt.153
  1.2 0.1 add.413
  1.4 0.1 add.423
  1.5 0.1 add.395
  1.6 0.8 copy.11
  2.4 0.1 reshape_squeeze.6
  2.5 0.1 dynamic-slice_bitcast_fusion.3
  2.6 0.1 reshape.485
  2.7 0.2 convert_reduce_fusion.1
  2.9 0.2 select_reduce_fusion.1
  3.1 0.1 reshape.486
  3.2 0.2 convert_reduce_fusion
  3.4 0.2 select_reduce_fusion
  3.7 0.1 reshape.488
  3.8 0.2 fusion
  4.0 0.2 convert_reduce_fusion.2
  4.3 0.1 select_n.177
  4.5 0.1 concatenate.26
  4.7 0.7 concatenate.27.list_ref
  5.3 111.0 %whole.1 = bf16[1024,128]{1,0:T(8,128)(2,1)} custom-call(s32[320]{0:T(512)} %concatenate.27.list_ref, bf16[1024,2048]{1,0:T(8,128)(2,1)} %bitcast.32, bf16[64,1024]{1,0:T(8,128)(2,1)} %w_ref.1, bf16[1024,128]{1,0:T(8,128)(2,1)} %fc_hbm.1, bf16[64,128,128]{2,1,0:T(8,128)(2,1)} %bitcast.33, bf16[8,128,128]{2,1,0:T(8,128)(2,1)} %bitcast.35, ...), custom_call_target="tpu_custom_call" | custom-call | tf_op jit(solution)/shard_map/whole/pallas_call | solution.py:348
  116.3 1.7 %copy.13 = bf16[1,1024,128]{2,1,0:T(8,128)(2,1)} copy(bf16[1,1024,128]{2,1,0:T(8,128)(2,1)} %bitcast.34) | data formatting | bytes 524288
  (22 shorter events, 0.7 us)

commit v2 on v1

--- a/solution.py
+++ b/solution.py
@@ -9,6 +9,7 @@
 
 MESH = pl.DeviceIdType.MESH
 CORES = 2
+LANES = 128
 PARTS = 4
 BF = jnp.bfloat16
 F32 = jnp.float32
@@ -32,7 +33,79 @@
     return lambda: pl.semaphore_wait(barrier, len(devices))
 
 
-def whole_kernel(tiles, cap, parts, hops, list_ref, x_hbm, w_ref, fc_hbm, adj_hbm, self_hbm, up_hbm, down_hbm, out_ref, *scratch):
+def make_lists(named_ref, counts_ref, table, chips, sizes, place):
+    tiles, cap, blocks, far = sizes
+    sx, z, oz, c = place
+    zs = tiles // CORES
+    kinds = 2 * far
+    span = 2 * cap
+    both = CORES * blocks
+    slots = named_ref.shape[0]
+    sends = blocks * slots
+
+    def iota(shape, axis):
+        return lax.broadcasted_iota(jnp.int32, shape, axis)
+
+    def receiver(kind, gz, gc):
+        gx = jnp.where(kind % 2 == 0, 1 - sx, sx)
+        return gx * tiles + (gz + 2 * (kind // 2)) % zs * CORES + gc
+
+    lane = iota((1, LANES), 1)
+    wide = (LANES, LANES)
+    entry = iota(wide, 0)
+    column = iota(wide, 1)
+    same_core = (entry // blocks) % CORES == (column // blocks) % CORES
+    limit = jnp.zeros((1, LANES), jnp.int32)
+    for b in range(blocks):
+        limit = jnp.where(lane % blocks == b, counts_ref[b], limit)
+    alive = (lane // both < limit) & ((lane // blocks) % CORES == c)
+    alive = jnp.where(alive, (lane % blocks) * slots + lane // both - sends, 0)
+    alive = jnp.transpose(jnp.broadcast_to(alive, wide))
+    for phase in range(2):
+        row = jnp.zeros((1, LANES), jnp.int32)
+        for slot in range(slots):
+            moved = pltpu.roll(named_ref[pl.ds(slot, 1), :], (slot * both - chips[phase] * both + LANES) % LANES, 1)
+            row = jnp.where(lane // both == slot, moved, row)
+        across = jnp.broadcast_to(row * LANES + lane, wide)
+        down = jnp.transpose(across)
+        named = down // LANES
+        less = across < down
+        order = jnp.sum(jnp.where(less, 1, 0), axis=1, keepdims=True)
+        rank = jnp.sum(jnp.where(less & same_core, 1, 0), axis=1, keepdims=True)
+        if phase == 0:
+            person = column // (kinds * cap)
+            kind = (column // cap) % kinds
+            core = jnp.where(person % 2 == 0, c, 1 - c)
+            want = receiver(kind, jnp.where(person < 2, z, oz), core) * cap + column % cap
+            packed = jnp.sum(jnp.where(rank == want, alive, 0), axis=0, keepdims=True)
+            table[pl.ds(0, 1), :] = packed + sends
+        kind = column // span % kinds
+        want = receiver(kind, z, c) * span + column % span
+        hit = order == want
+        core = (entry // blocks) % CORES
+        rank = jnp.clip(rank - named // blocks * cap, 0, cap - 1)
+        if phase == 0:
+            tile = core * (kinds * cap) + kind * cap + rank
+        else:
+            tile = jnp.where(kind < 2, core, core * (kinds - 2) + kind - 2) * cap + rank
+
+        def chosen(value):
+            return jnp.sum(jnp.where(hit, value, 0), axis=0, keepdims=True)
+
+        block = chosen(named % blocks)
+        table[pl.ds(1 + phase, 1), :] = chosen(tile)
+        table[pl.ds(3 + phase, 1), :] = chosen(entry % both)
+        again = (lane % span > 0) & (block == pltpu.roll(block, 1, 1))
+        table[pl.ds(5 + phase, 1), :] = jnp.where(again, 1, 0)
+        block = jnp.transpose(jnp.broadcast_to(block, wide))
+        fits = (entry // span == column // blocks) & (entry < kinds * span)
+        upto = jnp.sum(jnp.where(fits & (block <= column % blocks), 1, 0), axis=0, keepdims=True)
+        there = jnp.sum(jnp.where(fits & (block == column % blocks), 1, 0), axis=0, keepdims=True)
+        last = lane // blocks * span + upto - 1
+        table[pl.ds(7 + phase, 1), :] = jnp.where(there > 0, last, kinds * span)
+
+
+def whole_kernel(tiles, cap, parts, hops, counts_hbm, named_hbm, x_hbm, w_hbm, fc_hbm, adj_hbm, self_hbm, up_hbm, down_hbm, out_ref, *scratch):
     scratch = list(scratch)
 
     def take(count):
@@ -41,7 +114,8 @@
         return taken
 
     x_ref, fc_ref, w_all, acc, adj_ref, self_ref, up_ref, down_ref = take(8)
-    pack, adj_e, adj_l, run_e, run_l, state, agg, mine, send1, send2 = take(10)
+    table, lists, named_ref, counts_ref = take(4)
+    pack, adj_e, adj_x, adj_n, adj_f, run_e, run_l, state, agg, mine, send1, send2 = take(12)
     nodes_e, nodes_l = take(hops), take(hops)
     recv1, recv2 = take(2)
     ld, z_s, z_r, xy_s, xy_r, dg_s, dg_r, pt_s, pt_r = take(9)
@@ -49,7 +123,7 @@
 
     zs = tiles // CORES
     far = zs // 2
-    rows = w_ref.shape[0]
+    rows = w_hbm.shape[0]
     half = rows // 2
     blocks, tb, width = self_ref.shape[0], self_ref.shape[1], fc_ref.shape[1]
     sends = adj_ref.shape[0] - 1
@@ -81,31 +155,32 @@
     def arrived(dst, ss, rs, device):
         remote(dst, dst, ss, rs, device).wait_recv()
 
+    start = ((sx * tiles + t) * 2 + sy) * rows
     loads = [
         pltpu.make_async_copy(src, dst, ld.at[i])
         for i, (src, dst) in enumerate(
             (
+                (w_hbm, w_all.at[pl.ds(pl.multiple_of(start, rows), rows)]),
                 (adj_hbm, adj_ref.at[pl.ds(0, sends)]),
                 (x_hbm, x_ref),
                 (fc_hbm, fc_ref),
                 (self_hbm, self_ref),
                 (up_hbm, up_ref),
                 (down_hbm, down_ref),
+                (named_hbm, named_ref),
+                (counts_hbm, counts_ref),
             )
         )
     ]
     wait = greet([partner, xn, yn, zn, zp] + [zdev(j) for j in range(1, far)])
     for load in loads:
         load.start()
-    start = ((sx * tiles + t) * 2 + sy) * rows
-    w_all[pl.ds(pl.multiple_of(start, rows), rows)] = w_ref[...]
     adj_ref[sends] = jnp.zeros((tb, tb), BF)
     run_e[kinds * span] = jnp.zeros((tb, width), F32)
     run_l[kinds * span] = jnp.zeros((tb, width), F32)
+
+    loads[0].wait()
     wait()
-
-    def own(k):
-        return w_ref.at[pl.ds(k * half, half)]
 
     def at(x, m, core, y, k):
         first = ((x * tiles + places[m] * CORES + core) * 2 + y) * rows + k * half
@@ -113,22 +188,21 @@
 
     for k in range(2):
         for j in range(1, far):
-            go(own(k), at(sx, 0, c, sy, k), z_s.at[j, k], z_r.at[j, k], zdev(j))
+            go(at(sx, 0, c, sy, k), at(sx, 0, c, sy, k), z_s.at[j, k], z_r.at[j, k], zdev(j))
     for k in range(2):
-        go(own(k), at(sx, 0, c, sy, k), z_s.at[far, k], z_r.at[far, k], zn)
+        go(at(sx, 0, c, sy, k), at(sx, 0, c, sy, k), z_s.at[far, k], z_r.at[far, k], zn)
 
     def line(m, k):
         here = at(sx, m, c, sy, k)
-        src = here if m else own(k)
         if 0 < m < far:
             arrived(here, z_s.at[0, k], z_r.at[far - m, k], zdev(m))
         elif m:
             arrived(here, z_s.at[0, k], z_r.at[m, k], zn)
-        go(src, here, xy_s.at[0, m, k], xy_r.at[0, m, k], xn)
-        go(src, here, xy_s.at[1, m, k], xy_r.at[1, m, k], yn)
+        go(here, here, xy_s.at[0, m, k], xy_r.at[0, m, k], xn)
+        go(here, here, xy_s.at[1, m, k], xy_r.at[1, m, k], yn)
         if 0 < m < far:
-            go(src, here, z_s.at[far + m, k], z_r.at[far + m, k], zn)
-        go(src, here, pt_s.at[0, m, k], pt_r.at[0, m, k], partner)
+            go(here, here, z_s.at[far + m, k], z_r.at[far + m, k], zn)
+        go(here, here, pt_s.at[0, m, k], pt_r.at[0, m, k], partner)
 
     def cross(m, k):
         for kind, device, other, ref in (
@@ -147,35 +221,41 @@
 
     def pack_tiles():
         def keep(i, carry):
-            adj_e[i] = adj_ref[list_ref[i]]
+            adj_e[c * batch + i] = adj_ref[lists[0, i]]
             return carry
 
         def other(i, carry):
-            pack[i] = adj_ref[list_ref[batch + i]]
+            pack[i] = adj_ref[lists[0, batch + i]]
             return carry
 
         lax.fori_loop(0, batch, keep, 0, unroll=4)
         lax.fori_loop(0, 3 * batch, other, 0, unroll=4)
-        go(pack.at[pl.ds(0, batch)], adj_e.at[pl.ds(batch, batch)], aj_s.at[0, 0], aj_r.at[0, 0], partner)
-
-    bit = batch // 2
-
-    def send_tiles():
-        for piece in range(2):
-            for m, device in ((1, zn), (2, zp)):
-                go(
-                    pack.at[pl.ds(m * batch + piece * bit, bit)],
-                    adj_l.at[pl.ds((m - 1) * batch + piece * bit, bit)],
-                    aj_s.at[m, piece],
-                    aj_r.at[m, piece],
-                    device,
-                )
-
-    def nodes_out(hop, p):
-        first = p * per
-        here = nodes_e[hop].at[pl.ds(first, per)]
-        go(here, nodes_e[hop].at[pl.ds(blocks + first, per)], nd_s.at[hop, 0, p], nd_r.at[hop, 0, p], partner)
-        go(here, nodes_l[hop].at[pl.ds(first, per)], nd_s.at[hop, 1, p], nd_r.at[hop, 1, p], zn)
+        theirs = adj_e.at[pl.ds(pl.multiple_of(c * batch, batch), batch)]
+        go(pack.at[pl.ds(0, batch)], theirs, aj_s.at[0, 0], aj_r.at[0, 0], partner)
+
+    near = 2 * cap
+    stretch = ((adj_x, 0, cap), (adj_n, cap, cap), (adj_f, near, batch - near))
+
+    def send_tiles(piece):
+        into, first, size = stretch[piece]
+        for m, device in ((1, zn), (2, zp)):
+            there = into.at[pl.ds(pl.multiple_of(c * size, size), size)]
+            go(pack.at[pl.ds(m * batch + first, size)], there, aj_s.at[m, piece], aj_r.at[m, piece], device)
+
+    def tiles_in(piece):
+        into, first, size = stretch[piece]
+        for m, device, core in ((1, zn, c), (2, zp, oc)):
+            ref = into.at[pl.ds(pl.multiple_of(core * size, size), size)]
+            arrived(ref, aj_s.at[m, piece], aj_r.at[m, piece], device)
+
+    def seat(core, p):
+        return pl.ds(pl.multiple_of(core * blocks + p * per, per), per)
+
+    def nodes_out(hop, p, after):
+        here = nodes_e[hop].at[seat(c, p)]
+        here[...] = after.astype(BF).reshape(per, tb, width)
+        go(here, here, nd_s.at[hop, 0, p], nd_r.at[hop, 0, p], partner)
+        go(here, nodes_l[hop].at[seat(c, p)], nd_s.at[hop, 1, p], nd_r.at[hop, 1, p], zn)
 
     depth = CORES * 2 * rows
     tall = per * tb
@@ -205,8 +285,8 @@
             enc = jnp.maximum(product(strip) + acc[strip, :], 0.0).astype(BF)
             first = jnp.dot(enc, fc_ref[...], preferred_element_type=F32)
             state[strip, :] = first
-            nodes_e[0][pl.ds(p * per, per)] = first.astype(BF).reshape(per, tb, width)
-            nodes_out(0, p)
+            nodes_out(0, p, first)
+        send_tiles(1)
 
     steps = [(m, k) for m in range(zs) for k in range(2)]
     count = len(steps)
@@ -214,46 +294,53 @@
         if step < count:
             line(*steps[step])
         if step == 1:
-            loads[0].wait()
+            for load in loads[7:]:
+                load.wait()
+            make_lists(named_ref, counts_ref, table, [sx * zs + z, sx * zs + oz], (tiles, cap, blocks, far), (sx, z, oz, c))
+            spread = pltpu.make_async_copy(table, lists, ld.at[9])
+            spread.start()
+            loads[1].wait()
+            spread.wait()
             pack_tiles()
-        if step == 2 * far:
-            send_tiles()
+        if step == 2 * far - 1:
+            send_tiles(2)
+            send_tiles(0)
         if 0 <= step - 2 < count:
             cross(*steps[step - 2])
         if 0 <= step - 4 < count:
             corner(*steps[step - 4])
         if step == 5:
-            for load in loads[1:]:
+            for load in loads[2:7]:
                 load.wait()
         if 0 <= step - 5 < count and steps[step - 5][1]:
             multiply(steps[step - 5][0])
 
-    at_a, at_n, at_k, at_l = (4 * batch + i * 2 * kinds * span for i in range(4))
-
     def runs(phase, k, hop):
-        tiles_ref, nodes_ref, run = ((adj_e, nodes_e[hop], run_e), (adj_l, nodes_l[hop], run_l))[phase]
+        nodes_ref, run = ((nodes_e[hop], run_e), (nodes_l[hop], run_l))[phase]
+        tiles_ref = adj_e if phase == 0 else (adj_x, adj_n, adj_f)[min(k, 2)]
         total = None
         for i in range(span):
-            e = (phase * kinds + k) * span + i
-            one = jnp.dot(tiles_ref[list_ref[at_a + e]], nodes_ref[list_ref[at_n + e]], preferred_element_type=F32)
-            total = one if total is None else total * list_ref[at_k + e].astype(F32) + one
-            run[k * span + i] = total
+            e = k * span + i
+            tile, node = lists[1 + phase, e], lists[3 + phase, e]
+            one = jnp.dot(tiles_ref[tile], nodes_ref[node], preferred_element_type=F32)
+            total = one if total is None else total * lists[5 + phase, e].astype(F32) + one
+            run[e] = total
 
     def block_sum(k, r):
-        return run_e[list_ref[at_l + k * blocks + r]] + run_l[list_ref[at_l + (kinds + k) * blocks + r]]
+        return run_e[lists[7, k * blocks + r]] + run_l[lists[8, k * blocks + r]]
 
     waiting = []
     for hop in range(hops):
         def own_block(b, carry):
-            agg[b] = jnp.dot(self_ref[b], nodes_e[hop][b], preferred_element_type=F32)
+            agg[b] = jnp.dot(self_ref[b], nodes_e[hop][c * blocks + b], preferred_element_type=F32)
             return carry
 
         lax.fori_loop(0, blocks, own_block, 0, unroll=2)
         for p in range(parts):
-            ref = nodes_e[hop].at[pl.ds(blocks + p * per, per)]
+            ref = nodes_e[hop].at[seat(oc, p)]
             arrived(ref, nd_s.at[hop, 0, p], nd_r.at[hop, 0, p], partner)
         if hop == 0:
-            ref = adj_e.at[pl.ds(batch, batch)]
+            ref = adj_e.at[pl.ds(pl.multiple_of(oc * batch, batch), batch)]
             arrived(ref, aj_s.at[0, 0], aj_r.at[0, 0], partner)
 
         def early(k, carry):
@@ -262,16 +349,13 @@
 
         lax.fori_loop(0, kinds, early, 0)
         for p in range(parts):
-            ref = nodes_l[hop].at[pl.ds(p * per, per)]
+            ref = nodes_l[hop].at[seat(c, p)]
             arrived(ref, nd_s.at[hop, 1, p], nd_r.at[hop, 1, p], zn)
-            go(ref, nodes_l[hop].at[pl.ds(blocks + p * per, per)], nd_s.at[hop, 2, p], nd_r.at[hop, 2, p], partner)
+            go(ref, ref, nd_s.at[hop, 2, p], nd_r.at[hop, 2, p], partner)
         if hop == 0:
-            for piece in range(2):
-                for m, device in ((1, zn), (2, zp)):
-                    ref = adj_l.at[pl.ds((m - 1) * batch + piece * bit, bit)]
-                    arrived(ref, aj_s.at[m, piece], aj_r.at[m, piece], device)
+            tiles_in(2)
         for p in range(parts):
-            ref = nodes_l[hop].at[pl.ds(blocks + p * per, per)]
+            ref = nodes_l[hop].at[seat(oc, p)]
             arrived(ref, nd_s.at[hop, 2, p], nd_r.at[hop, 2, p], partner)
 
         for copy in waiting:
@@ -296,16 +380,20 @@
             runs(1, 2 * j + 1, hop)
             for r in range(blocks):
                 mine[j - 1, r] = block_sum(2 * j + 1, r)
+        if hop == 0:
+            tiles_in(0)
         across(0, 0)
-        runs(1, 1, hop)
-        for r in range(blocks):
-            agg[r] += block_sum(1, r)
         for p in range(parts):
             piece = pl.ds(p * per, per)
             for j in range(1, far):
                 crossed(j, p)
                 send2[j - 1, piece] = (mine[j - 1, piece] + recv1[hop, j, piece].astype(F32)).astype(BF)
                 go(send2.at[j - 1, piece], recv2.at[hop, j - 1, piece], s2.at[hop, j - 1, p], r2.at[hop, j - 1, p], zdev(j), waiting)
+        if hop == 0:
+            tiles_in(1)
+        runs(1, 1, hop)
+        for r in range(blocks):
+            agg[r] += block_sum(1, r)
         for p in range(parts):
             piece = pl.ds(p * per, per)
             strip = pl.ds(p * tall, tall)
@@ -322,13 +410,12 @@
                 out_ref[strip, :] = after.astype(BF)
             else:
                 state[strip, :] = after
-                nodes_e[hop + 1][piece] = after.astype(BF).reshape(per, tb, width)
-                nodes_out(hop + 1, p)
+                nodes_out(hop + 1, p, after)
     for copy in started + waiting:
         copy.wait_send()
 
 
-def fused(rows, w_proj, w_fc, w_up, w_down, self_adj, adjacency, lists, cap):
+def fused(rows, w_proj, w_fc, w_up, w_down, self_adj, adjacency, named, counts, cap):
     tiles = lax.axis_size("tile")
     zs = tiles // CORES
     far = zs // 2
@@ -345,10 +432,11 @@
     dma = pltpu.SemaphoreType.DMA
     tile = (tb, tb)
     piece = (blocks, tb, width)
+    held = (counts, named, rows, w_proj, w_fc, adjacency.reshape((blocks * slots,) + tile), self_adj, w_up, w_down)
     return pl.pallas_call(
         functools.partial(whole_kernel, tiles, cap, parts, hops),
         out_shape=jax.ShapeDtypeStruct((rows.shape[0], width), BF),
-        in_specs=[pl.BlockSpec(memory_space=pltpu.SMEM), hbm, vmem] + [hbm] * 5,
+        in_specs=[hbm] * 9,
         out_specs=vmem,
         scratch_shapes=[
             pltpu.VMEM(rows.shape, BF),
@@ -359,9 +447,15 @@
             pltpu.VMEM(self_adj.shape, BF),
             pltpu.VMEM(w_up.shape, BF),
             pltpu.VMEM(w_down.shape, BF),
+            pltpu.VMEM((16, LANES), jnp.int32),
+            pltpu.SMEM((16, LANES), jnp.int32),
+            pltpu.VMEM(named.shape, jnp.int32),
+            pltpu.SMEM(counts.shape, jnp.int32),
             pltpu.VMEM((3 * batch,) + tile, BF),
             pltpu.VMEM((2 * batch,) + tile, BF),
-            pltpu.VMEM((2 * batch,) + tile, BF),
+            pltpu.VMEM((2 * cap,) + tile, BF),
+            pltpu.VMEM((2 * cap,) + tile, BF),
+            pltpu.VMEM((2 * batch - 4 * cap,) + tile, BF),
             pltpu.VMEM((kinds * span + 1, tb, width), F32),
             pltpu.VMEM((kinds * span + 1, tb, width), F32),
             pltpu.VMEM((rows.shape[0], width), F32),
@@ -372,80 +466,20 @@
         ]
         + [pltpu.VMEM((2 * blocks, tb, width), BF)] * (2 * hops)
         + [pltpu.VMEM((hops, far) + piece, BF), pltpu.VMEM((hops, distant) + piece, BF)]
-        + [dma((6,))]
+        + [dma((10,))]
         + [dma((zs, 2))] * 2
         + [dma((2, zs, 2))] * 2
         + [dma((zs, 2))] * 2
         + [dma((4, zs, 2))] * 2
-        + [dma((3, 2))] * 2
+        + [dma((3, 3))] * 2
         + [dma((hops, 3, parts))] * 2
         + [dma((hops, far, parts))] * 2
         + [dma((hops, distant, parts))] * 2,
         compiler_params=pltpu.CompilerParams(
-            collective_id=0, has_side_effects=True, vmem_limit_bytes=62 << 20
+            collective_id=0, has_side_effects=True, vmem_limit_bytes=48 << 20
         ),
         name="whole",
-    )(lists, rows, w_proj, w_fc, adjacency.reshape((blocks * slots,) + tile), self_adj, w_up, w_down)
-
-
-def tile_lists(neighbours, counts, slots, cap):
-    tiles = lax.axis_size("tile")
-    zs = tiles // CORES
-    far = zs // 2
-    kinds = 2 * far
-    span = 2 * cap
-    blocks = counts.shape[0]
-    sends = blocks * slots
-    x = lax.axis_index("section")
-    t = lax.axis_index("tile")
-    z, c = t // CORES, t % CORES
-    oz = z + 1 - 2 * (z % 2)
-    seats = [(z, c), (z, 1 - c), (oz, c), (oz, 1 - c)]
-    entries = neighbours.reshape(-1)
-
-    def group(gx, gz, gc):
-        return gx * tiles + gz * CORES + gc
-
-    def receivers(seat):
-        gz, gc = seat
-        return [group(gx, (gz + 2 * j) % zs, gc) for j in range(far) for gx in (1 - x, x)]
-
-    named = jnp.stack(
-        [lax.dynamic_slice_in_dim(entries, group(x, gz, gc) * sends, sends) for gz, gc in seats]
-    )
-    place = jnp.arange(sends, dtype=jnp.int32)
-    key = named * sends + place
-    rank = jnp.sum((key[:, None, :] < key[:, :, None]).astype(jnp.int32), axis=2)
-    live = (jnp.arange(slots, dtype=jnp.int32)[None, :] < counts[:, None]).reshape(sends)
-    wanted = jnp.stack([g for seat in seats for g in receivers(seat)])
-    wanted = (wanted[:, None] * cap + jnp.arange(cap, dtype=jnp.int32)[None, :]).reshape(-1)
-    hit = (wanted[:, None] == rank[0][None, :]) & live[None, :]
-    packed = sends + jnp.sum(jnp.where(hit, place[None, :] - sends, 0), axis=1)
-
-    both = named.reshape(2, 2 * sends)
-    seat_of = jnp.arange(2 * sends, dtype=jnp.int32) // sends
-    key = both * (2 * sends) + jnp.arange(2 * sends, dtype=jnp.int32)
-    order = jnp.sum((key[:, None, :] < key[:, :, None]).astype(jnp.int32), axis=2)
-    tile_at = seat_of * (kinds * cap) + rank.reshape(2, 2 * sends) - (both // blocks) * cap
-    node_at = jnp.arange(2 * sends, dtype=jnp.int32) // slots
-    code = ((tile_at * (2 * blocks)) + node_at) * blocks + both % blocks
-    mine = jnp.stack(receivers(seats[0]))
-    ask = (mine[:, None] * span + jnp.arange(span, dtype=jnp.int32)[None, :]).reshape(-1)
-    hit = ask[None, :, None] == order[:, None, :]
-    code = jnp.sum(jnp.where(hit, code[:, None, :], 0), axis=2).reshape(2, kinds, span)
-    block = code % blocks
-    node = (code // blocks) % (2 * blocks)
-    kind = jnp.arange(kinds, dtype=jnp.int32)[None, :, None]
-    tile = code // (2 * blocks * blocks) + kind * cap
-    first = jnp.arange(span, dtype=jnp.int32)[None, None, :] > 0
-    same = first & (block == jnp.roll(block, 1, axis=2))
-    want = jnp.arange(blocks, dtype=jnp.int32)[None, None, :, None]
-    upto = jnp.sum((block[:, :, None, :] <= want).astype(jnp.int32), axis=3)
-    there = jnp.any(block[:, :, None, :] == want, axis=3)
-    last = jnp.where(there, kind * span + upto - 1, kinds * span)
-    return jnp.concatenate(
-        [packed, tile.reshape(-1), node.reshape(-1), same.astype(jnp.int32).reshape(-1), last.reshape(-1)]
-    )
+    )(*(pltpu.with_memory_space_constraint(a, pltpu.HBM) for a in held))
 
 
 def local(features, w_proj, w_fc, w_up, w_down, self_adj, adjacency, nbr_block, counts):
@@ -462,9 +496,9 @@
     live = jnp.arange(slots, dtype=jnp.int32)[None, :] < counts[0][:, None]
     square = lax.axis_size("section") == 2 and lax.axis_size("slide") == 2
     pairs = lax.axis_size("tile") % (2 * CORES) == 0
-    if square and pairs and sends == peers * cap and w_proj.shape[0] % 32 == 0:
-        lists = tile_lists(nbr_block[0], counts[0], slots, cap)
-        return fused(rows, w_proj, w_fc, w_up, w_down, self_adj[0], adjacency[0], lists, cap)[None]
+    lanes = nbr_block.shape[1] == LANES and 2 * sends == LANES
+    if square and pairs and lanes and sends == peers * cap and w_proj.shape[0] % 32 == 0:
+        return fused(rows, w_proj, w_fc, w_up, w_down, self_adj[0], adjacency[0], nbr_block[0].T, counts[0], cap)[None]
     pre = jnp.dot(
         rows,
         lax.all_gather(w_proj, ("section", "tile", "slide"), axis=0, tiled=True),

time: 118 us -> 106 us (0.90)
  Pallas kernels: 111 us -> 105 us
  local copies, waits for them, and re-layouts: 4.49 us -> 0.71 us
  other arithmetic: 2.43 us -> 0 us
    pallas_call x1, Pallas kernels: 111 us -> 105 us  [fused(): pl.pallas_call(functools.partial(whole_kernel, tiles, cap, parts, hops),...]
    unnamed x2 -> x1, local copies, waits for them, and re-layouts: 2.46 us -> 0.71 us
where the time goes in v2:
time: 106 us; the launch traced here: 105 us
  Pallas kernels  105 us (99%)
    pallas_call x1, Pallas kernels, fused(): pl.pallas_call(functools.partial(whole_kernel, tiles, cap, parts, hops),...  105 us

profile of v2, /device:TPU:0, one launch (start us, length us, event | category | flops | bytes accessed | tf_op | source)
XLA Modules:
  0.0 105.5 jit_solution(13998825290850735816)
XLA Ops:
  0.0 104.8 %whole.1 = bf16[1024,128]{1,0:T(8,128)(2,1)S(1)} custom-call(s32[8]{0:T(128)} %bitcast.13, s32[8,128]{1,0:T(8,128)} %bitcast.12, bf16[1024,2048]{1,0:T(8,128)(2,1)} %bitcast.9, bf16[64,1024]{1,0:T(8,128)(2,1)} %w_hbm.1, bf16[1024,128]{1,0:T(8,128)(2,1)} %fc_hbm.1, bf16[64,128,128]{2,1,0:T(8,128)(2,1)} %bitcast.10, bf16[8,128,128]{2,1,0:T(8,128)(2,1)} %bitcast.11, ...), custom_call_target="tpu_custom_call" | custom-call | tf_op jit(solution)/shard_map/whole/pallas_call | solution.py:436
  104.8 0.7 copy.11

commit v3 on v2

--- a/solution.py
+++ b/solution.py
@@ -10,7 +10,11 @@
 MESH = pl.DeviceIdType.MESH
 CORES = 2
 LANES = 128
-PARTS = 4
+SPLIT = True
+WINDOW = 4
+NODE_SHARES = (2, 2, 2, 1, 1)
+SUM_SHARES = (1, 1, 1, 1, 1, 1, 1, 1)
+CUTS = 2
 BF = jnp.bfloat16
 F32 = jnp.float32
 
@@ -105,7 +109,37 @@
         table[pl.ds(7 + phase, 1), :] = jnp.where(there > 0, last, kinds * span)
 
 
-def whole_kernel(tiles, cap, parts, hops, counts_hbm, named_hbm, x_hbm, w_hbm, fc_hbm, adj_hbm, self_hbm, up_hbm, down_hbm, out_ref, *scratch):
+def cut(blocks, shares):
+    unit = blocks // 8 if blocks % 8 == 0 else 0
+    sizes = [unit * share for share in shares] if unit else [blocks]
+    return [(sum(sizes[:i]), size) for i, size in enumerate(sizes)]
+
+
+def node_parts(blocks):
+    return cut(blocks, NODE_SHARES)
+
+
+def sum_parts(blocks):
+    return cut(blocks, SUM_SHARES)
+
+
+def schedule(zs, parts):
+    steps = [(m, k) for m in range(zs) for k in range(CUTS)]
+    plan = [(1, 1, "lists"), (1, 2, "pack"), (CUTS * (zs // 2) - 1, 1, "tiles"), (5, 5, "ready")]
+    for i, (m, k) in enumerate(steps):
+        plan += [(i, 0, "line", m, k), (i + 2, 3, "cross", m, k), (i + 4, 4, "corner", m, k)]
+        if k < CUTS - 1:
+            continue
+        for p in range(parts):
+            if m < zs - 1 or not SPLIT:
+                plan.append((i + 5, 6, "multiply", m, p, (0, 1)))
+            else:
+                plan.append((i + 4, 6, "multiply", m, p, (0,)))
+                plan.append((i + 5, 6, "multiply", m, p, (1,)))
+    return [act[2:] for act in sorted(plan, key=lambda act: act[:2])]
+
+
+def whole_kernel(tiles, cap, hops, counts_hbm, named_hbm, x_hbm, w_hbm, fc_hbm, adj_hbm, self_hbm, up_hbm, down_hbm, out_ref, *scratch):
     scratch = list(scratch)
 
     def take(count):
@@ -124,13 +158,13 @@
     zs = tiles // CORES
     far = zs // 2
     rows = w_hbm.shape[0]
-    half = rows // 2
+    half = rows // CUTS
     blocks, tb, width = self_ref.shape[0], self_ref.shape[1], fc_ref.shape[1]
     sends = adj_ref.shape[0] - 1
     kinds = 2 * far
     batch = kinds * cap
     span = 2 * cap
-    per = blocks // parts
+    outs, sums = node_parts(blocks), sum_parts(blocks)
     sx = lax.axis_index("section")
     sy = lax.axis_index("slide")
     t = lax.axis_index("tile")
@@ -186,11 +220,12 @@
         first = ((x * tiles + places[m] * CORES + core) * 2 + y) * rows + k * half
         return w_all.at[pl.ds(pl.multiple_of(first, half), half)]
 
-    for k in range(2):
+    mine_at = [at(sx, 0, c, sy, k) for k in range(CUTS)]
+    for k in range(CUTS):
         for j in range(1, far):
-            go(at(sx, 0, c, sy, k), at(sx, 0, c, sy, k), z_s.at[j, k], z_r.at[j, k], zdev(j))
-    for k in range(2):
-        go(at(sx, 0, c, sy, k), at(sx, 0, c, sy, k), z_s.at[far, k], z_r.at[far, k], zn)
+            go(mine_at[k], mine_at[k], z_s.at[j, k], z_r.at[j, k], zdev(j))
+    for k in range(CUTS):
+        go(mine_at[k], mine_at[k], z_s.at[far, k], z_r.at[far, k], zn)
 
     def line(m, k):
         here = at(sx, m, c, sy, k)
@@ -210,13 +245,13 @@
             (1, yn, xn, at(sx, m, c, oy, k)),
         ):
             arrived(ref, xy_s.at[kind, m, k], xy_r.at[kind, m, k], device)
-            if k == kind:
+            if k % 2 == kind:
                 go(ref, ref, dg_s.at[m, k], dg_r.at[m, k], other)
             go(ref, ref, pt_s.at[1 + kind, m, k], pt_r.at[1 + kind, m, k], partner)
 
     def corner(m, k):
         ref = at(ox, m, c, oy, k)
-        arrived(ref, dg_s.at[m, k], dg_r.at[m, k], (yn, xn)[k])
+        arrived(ref, dg_s.at[m, k], dg_r.at[m, k], (yn, xn)[k % 2])
         go(ref, ref, pt_s.at[3, m, k], pt_r.at[3, m, k], partner)
 
     def pack_tiles():
@@ -249,71 +284,68 @@
             arrived(ref, aj_s.at[m, piece], aj_r.at[m, piece], device)
 
     def seat(core, p):
-        return pl.ds(pl.multiple_of(core * blocks + p * per, per), per)
+        return pl.ds(core * blocks + outs[p][0], outs[p][1])
+
+    def strip_of(p):
+        return pl.ds(outs[p][0] * tb, outs[p][1] * tb)
 
     def nodes_out(hop, p, after):
         here = nodes_e[hop].at[seat(c, p)]
-        here[...] = after.astype(BF).reshape(per, tb, width)
+        here[...] = after.astype(BF).reshape(outs[p][1], tb, width)
         go(here, here, nd_s.at[hop, 0, p], nd_r.at[hop, 0, p], partner)
         go(here, nodes_l[hop].at[seat(c, p)], nd_s.at[hop, 1, p], nd_r.at[hop, 1, p], zn)
+        if p == len(outs) - 1:
+            go(here, nodes_l[hop].at[seat(c, p)], nd_s.at[hop, 2, p], nd_r.at[hop, 2, p], zp)
 
     depth = CORES * 2 * rows
-    tall = per * tb
-
-    def multiply(m):
-        for k in range(2):
-            for kind, (x, y) in enumerate(((sx, sy), (ox, sy), (sx, oy), (ox, oy))):
-                arrived(at(x, m, oc, y, k), pt_s.at[kind, m, k], pt_r.at[kind, m, k], partner)
-        slabs = [pl.ds(pl.multiple_of((x * zs + places[m]) * depth, depth), depth) for x in (sx, ox)]
-
-        def product(strip):
-            total = jnp.dot(x_ref[strip, slabs[0]], w_all[slabs[0], :], preferred_element_type=F32)
-            return total + jnp.dot(x_ref[strip, slabs[1]], w_all[slabs[1], :], preferred_element_type=F32)
-
-        if m < zs - 1:
-
-            def body(i, carry):
-                strip = pl.ds(pl.multiple_of(i * tall, tall), tall)
-                total = product(strip)
-                acc[strip, :] = total + acc[strip, :] if m else total
-                return carry
-
-            lax.fori_loop(0, parts, body, 0)
+
+    def multiply(m, p, sides):
+        if p == 0:
+            for k in range(CUTS):
+                for kind, (x, y, side) in enumerate(((sx, sy, 0), (ox, sy, 1), (sx, oy, 0), (ox, oy, 1))):
+                    if side not in sides:
+                        continue
+                    arrived(at(x, m, oc, y, k), pt_s.at[kind, m, k], pt_r.at[kind, m, k], partner)
+        strip = strip_of(p)
+        total = acc[strip, :] if m or 0 not in sides else None
+        for side in sides:
+            slab = pl.ds(pl.multiple_of(((sx, ox)[side] * zs + places[m]) * depth, depth), depth)
+            one = jnp.dot(x_ref[strip, slab], w_all[slab, :], preferred_element_type=F32)
+            total = one if total is None else total + one
+        if m < zs - 1 or 1 not in sides:
+            acc[strip, :] = total
             return
-        for p in range(parts):
-            strip = pl.ds(p * tall, tall)
-            enc = jnp.maximum(product(strip) + acc[strip, :], 0.0).astype(BF)
-            first = jnp.dot(enc, fc_ref[...], preferred_element_type=F32)
-            state[strip, :] = first
-            nodes_out(0, p, first)
-        send_tiles(1)
-
-    steps = [(m, k) for m in range(zs) for k in range(2)]
-    count = len(steps)
-    for step in range(count + 5):
-        if step < count:
-            line(*steps[step])
-        if step == 1:
-            for load in loads[7:]:
-                load.wait()
-            make_lists(named_ref, counts_ref, table, [sx * zs + z, sx * zs + oz], (tiles, cap, blocks, far), (sx, z, oz, c))
-            spread = pltpu.make_async_copy(table, lists, ld.at[9])
-            spread.start()
-            loads[1].wait()
-            spread.wait()
-            pack_tiles()
-        if step == 2 * far - 1:
-            send_tiles(2)
-            send_tiles(0)
-        if 0 <= step - 2 < count:
-            cross(*steps[step - 2])
-        if 0 <= step - 4 < count:
-            corner(*steps[step - 4])
-        if step == 5:
-            for load in loads[2:7]:
-                load.wait()
-        if 0 <= step - 5 < count and steps[step - 5][1]:
-            multiply(steps[step - 5][0])
+        enc = jnp.maximum(total, 0.0).astype(BF)
+        first = jnp.dot(enc, fc_ref[...], preferred_element_type=F32)
+        state[strip, :] = first
+        nodes_out(0, p, first)
+        if p == len(outs) - 1:
+            send_tiles(1)
+
+    spread = pltpu.make_async_copy(table, lists, ld.at[9])
+
+    def index_lists():
+        for load in loads[7:]:
+            load.wait()
+        make_lists(named_ref, counts_ref, table, [sx * zs + z, sx * zs + oz], (tiles, cap, blocks, far), (sx, z, oz, c))
+        spread.start()
+
+    def packing():
+        loads[1].wait()
+        spread.wait()
+        pack_tiles()
+
+    def ready():
+        for load in loads[2:7]:
+            load.wait()
+
+    def tiles_out():
+        send_tiles(2)
+        send_tiles(0)
+
+    acts = {"line": line, "cross": cross, "corner": corner, "multiply": multiply, "lists": index_lists, "pack": packing, "tiles": tiles_out, "ready": ready}
+    for act, *where in schedule(zs, len(outs)):
+        acts[act](*where)
 
     def runs(phase, k, hop):
         nodes_ref, run = ((nodes_e[hop], run_e), (nodes_l[hop], run_l))[phase]
@@ -329,6 +361,12 @@
     def block_sum(k, r):
         return run_e[lists[7, k * blocks + r]] + run_l[lists[8, k * blocks + r]]
 
+    def forward(hop, p):
+        ref = nodes_l[hop].at[seat(c, p)]
+        arrived(ref, nd_s.at[hop, 1, p], nd_r.at[hop, 1, p], zn)
+        if p < len(outs) - 1:
+            go(ref, ref, nd_s.at[hop, 2, p], nd_r.at[hop, 2, p], partner)
+
     waiting = []
     for hop in range(hops):
         def own_block(b, carry):
@@ -336,7 +374,7 @@
             return carry
 
         lax.fori_loop(0, blocks, own_block, 0, unroll=2)
-        for p in range(parts):
+        for p in range(len(outs)):
             ref = nodes_e[hop].at[seat(oc, p)]
             arrived(ref, nd_s.at[hop, 0, p], nd_r.at[hop, 0, p], partner)
         if hop == 0:
@@ -348,13 +386,11 @@
             return carry
 
         lax.fori_loop(0, kinds, early, 0)
-        for p in range(parts):
-            ref = nodes_l[hop].at[seat(c, p)]
-            arrived(ref, nd_s.at[hop, 1, p], nd_r.at[hop, 1, p], zn)
-            go(ref, ref, nd_s.at[hop, 2, p], nd_r.at[hop, 2, p], partner)
+        for p in range(len(outs)):
+            forward(hop, p)
         if hop == 0:
             tiles_in(2)
-        for p in range(parts):
+        for p in range(len(outs)):
             ref = nodes_l[hop].at[seat(oc, p)]
             arrived(ref, nd_s.at[hop, 2, p], nd_r.at[hop, 2, p], partner)
 
@@ -364,14 +400,14 @@
 
         def across(j, k):
             runs(1, k, hop)
-            for p in range(parts):
-                for r in range(p * per, p * per + per):
+            for p, (first, size) in enumerate(sums):
+                for r in range(first, first + size):
                     send1[j, r] = block_sum(k, r).astype(BF)
-                piece = pl.ds(p * per, per)
+                piece = pl.ds(first, size)
                 go(send1.at[j, piece], recv1.at[hop, j, piece], s1.at[hop, j, p], r1.at[hop, j, p], xn, waiting)
 
         def crossed(j, p):
-            ref = recv1.at[hop, j, pl.ds(p * per, per)]
+            ref = recv1.at[hop, j, pl.ds(*sums[p])]
             arrived(ref, s1.at[hop, j, p], r1.at[hop, j, p], xn)
 
         for j in range(1, far):
@@ -383,26 +419,36 @@
         if hop == 0:
             tiles_in(0)
         across(0, 0)
-        for p in range(parts):
-            piece = pl.ds(p * per, per)
+        def relay(p):
+            piece = pl.ds(*sums[p])
             for j in range(1, far):
                 crossed(j, p)
                 send2[j - 1, piece] = (mine[j - 1, piece] + recv1[hop, j, piece].astype(F32)).astype(BF)
                 go(send2.at[j - 1, piece], recv2.at[hop, j - 1, piece], s2.at[hop, j - 1, p], r2.at[hop, j - 1, p], zdev(j), waiting)
+
+        for p in range(min(WINDOW, len(sums))):
+            relay(p)
         if hop == 0:
             tiles_in(1)
         runs(1, 1, hop)
         for r in range(blocks):
             agg[r] += block_sum(1, r)
-        for p in range(parts):
-            piece = pl.ds(p * per, per)
-            strip = pl.ds(p * tall, tall)
-            crossed(0, p)
+        for p, (first, size) in enumerate(outs):
+            piece = pl.ds(first, size)
+            strip = strip_of(p)
+            for q, (begin, length) in enumerate(sums):
+                if not first <= begin < first + size:
+                    continue
+                crossed(0, q)
+                for j in range(1, far):
+                    ref = recv2.at[hop, j - 1, pl.ds(begin, length)]
+                    arrived(ref, s2.at[hop, j - 1, q], r2.at[hop, j - 1, q], zdev(j))
+                if q + WINDOW < len(sums):
+                    relay(q + WINDOW)
             total = agg[piece] + recv1[hop, 0, piece].astype(F32)
             for j in range(1, far):
-                arrived(recv2.at[hop, j - 1, piece], s2.at[hop, j - 1, p], r2.at[hop, j - 1, p], zdev(j))
                 total += recv2[hop, j - 1, piece].astype(F32)
-            gathered = total.astype(BF).reshape(tall, width)
+            gathered = total.astype(BF).reshape(size * tb, width)
             inner = jnp.dot(gathered, up_ref[hop], preferred_element_type=F32)
             inner = jnp.maximum(inner, 0.0).astype(BF)
             after = state[strip, :] + jnp.dot(inner, down_ref[hop], preferred_element_type=F32)
@@ -422,7 +468,7 @@
     blocks, slots, tb, _ = adjacency.shape
     width = w_fc.shape[1]
     hops = w_up.shape[0]
-    parts = PARTS if blocks % PARTS == 0 else 1
+    parts, pieces = len(node_parts(blocks)), len(sum_parts(blocks))
     kinds = 2 * far
     batch = kinds * cap
     span = 2 * cap
@@ -434,7 +480,7 @@
     piece = (blocks, tb, width)
     held = (counts, named, rows, w_proj, w_fc, adjacency.reshape((blocks * slots,) + tile), self_adj, w_up, w_down)
     return pl.pallas_call(
-        functools.partial(whole_kernel, tiles, cap, parts, hops),
+        functools.partial(whole_kernel, tiles, cap, hops),
         out_shape=jax.ShapeDtypeStruct((rows.shape[0], width), BF),
         in_specs=[hbm] * 9,
         out_specs=vmem,
@@ -467,14 +513,14 @@
         + [pltpu.VMEM((2 * blocks, tb, width), BF)] * (2 * hops)
         + [pltpu.VMEM((hops, far) + piece, BF), pltpu.VMEM((hops, distant) + piece, BF)]
         + [dma((10,))]
-        + [dma((zs, 2))] * 2
-        + [dma((2, zs, 2))] * 2
-        + [dma((zs, 2))] * 2
-        + [dma((4, zs, 2))] * 2
+        + [dma((zs, CUTS))] * 2
+        + [dma((2, zs, CUTS))] * 2
+        + [dma((zs, CUTS))] * 2
+        + [dma((4, zs, CUTS))] * 2
         + [dma((3, 3))] * 2
         + [dma((hops, 3, parts))] * 2
-        + [dma((hops, far, parts))] * 2
-        + [dma((hops, distant, parts))] * 2,
+        + [dma((hops, far, pieces))] * 2
+        + [dma((hops, distant, pieces))] * 2,
         compiler_params=pltpu.CompilerParams(
             collective_id=0, has_side_effects=True, vmem_limit_bytes=48 << 20
         ),

time: 106 us -> 102 us (0.962)
  Pallas kernels: 105 us -> 101 us
    pallas_call x1, Pallas kernels: 105 us -> 101 us  [fused(): pl.pallas_call(functools.partial(whole_kernel, tiles, cap, hops), out_sha...]
where the time goes in v3:
time: 102 us
  Pallas kernels  101 us (99%)
    pallas_call x1, Pallas kernels, fused(): pl.pallas_call(functools.partial(whole_kernel, tiles, cap, hops), out_sha...  101 us

profile of v3, /device:TPU:0, one launch (start us, length us, event | category | flops | bytes accessed | tf_op | source)
XLA Modules:
  0.0 102.1 jit_solution(10490244592401358348)
XLA Ops:
  0.0 101.4 %whole.1 = bf16[1024,128]{1,0:T(8,128)(2,1)S(1)} custom-call(s32[8]{0:T(128)} %bitcast.13, s32[8,128]{1,0:T(8,128)} %bitcast.12, bf16[1024,2048]{1,0:T(8,128)(2,1)} %bitcast.9, bf16[64,1024]{1,0:T(8,128)(2,1)} %w_hbm.1, bf16[1024,128]{1,0:T(8,128)(2,1)} %fc_hbm.1, bf16[64,128,128]{2,1,0:T(8,128)(2,1)} %bitcast.10, bf16[8,128,128]{2,1,0:T(8,128)(2,1)} %bitcast.11, ...), custom_call_target="tpu_custom_call" | custom-call | tf_op jit(solution)/shard_map/whole/pallas_call | solution.py:482
  101.4 0.7 copy.11

commit v4 on v3

--- a/solution.py
+++ b/solution.py
@@ -373,7 +373,6 @@
             agg[b] = jnp.dot(self_ref[b], nodes_e[hop][c * blocks + b], preferred_element_type=F32)
             return carry
 
-        lax.fori_loop(0, blocks, own_block, 0, unroll=2)
         for p in range(len(outs)):
             ref = nodes_e[hop].at[seat(oc, p)]
             arrived(ref, nd_s.at[hop, 0, p], nd_r.at[hop, 0, p], partner)
@@ -385,7 +384,7 @@
             runs(0, k, hop)
             return carry
 
-        lax.fori_loop(0, kinds, early, 0)
+        lax.fori_loop(2, kinds, early, 0)
         for p in range(len(outs)):
             forward(hop, p)
         if hop == 0:
@@ -416,6 +415,8 @@
             runs(1, 2 * j + 1, hop)
             for r in range(blocks):
                 mine[j - 1, r] = block_sum(2 * j + 1, r)
+        lax.fori_loop(0, 2, early, 0)
+        lax.fori_loop(0, blocks, own_block, 0, unroll=2)
         if hop == 0:
             tiles_in(0)
         across(0, 0)

time: 102 us -> 102 us (level)
  no operation moved by 1% of the time
where the time goes in v4:
time: 102 us
  Pallas kernels  101 us (99%)
    pallas_call x1, Pallas kernels, fused(): pl.pallas_call(functools.partial(whole_kernel, tiles, cap, hops), out_sha...  101 us

profile of v4, /device:TPU:0, one launch (start us, length us, event | category | flops | bytes accessed | tf_op | source)
XLA Modules:
  0.0 101.9 jit_solution(12855151529249090095)
XLA Ops:
  0.0 101.2 %whole.1 = bf16[1024,128]{1,0:T(8,128)(2,1)S(1)} custom-call(s32[8]{0:T(128)} %bitcast.13, s32[8,128]{1,0:T(8,128)} %bitcast.12, bf16[1024,2048]{1,0:T(8,128)(2,1)} %bitcast.9, bf16[64,1024]{1,0:T(8,128)(2,1)} %w_hbm.1, bf16[1024,128]{1,0:T(8,128)(2,1)} %fc_hbm.1, bf16[64,128,128]{2,1,0:T(8,128)(2,1)} %bitcast.10, bf16[8,128,128]{2,1,0:T(8,128)(2,1)} %bitcast.11, ...), custom_call_target="tpu_custom_call" | custom-call | tf_op jit(solution)/shard_map/whole/pallas_call | solution.py:483
  101.2 0.7 copy.11
